TPU v7x, 32 devices: a whole 2x2x4 slice. The times are simulated.
32 devices in a mesh: groups: 1, pts: 32 (over z, y, x, core).
Axes of the slice: x: 2, y: 2, z: 4, core: 2. Of those that a mesh axis runs over, the one named last changes fastest.
Arguments:
- residual_cols: bfloat16 [16384, 256], P(('groups', 'pts')), may hold values from -6 to 6
- leaf_inverse: bfloat16 [16384, 128], P(('groups', 'pts'))
- basis_left: float32 [7, 16384, 128], P(None, ('groups', 'pts')), may hold values from -0.15625 to 0.15625
- basis_right: float32 [7, 16384, 128], P(None, ('groups', 'pts'))
- point_pos: float32 [16384], replicated, may hold values from 0 to 16, as said below
- map_pos: float32 [2048], P('pts'), may hold values from 0 to 16, as said below
- prior_map: bfloat16 [2048, 256], P(('groups', 'pts')), may hold values from -6 to 6
- block_first: int32 [32, 32], replicated, may hold values from 0 to 2, as said below
- block_count: int32 [32, 32], replicated, may hold values from 0 to 2, as said below
Outputs:
- solved_cols: float32 [16384, 256], P(('groups', 'pts'))
- sample_map: float32 [2048, 256], P(('groups', 'pts'))
Inputs may be any that keep to these rules, and one draw needn't show every extreme that they name: `block_count`: at most 2; the listed blocks of tile d from source s include every block of s that has a point within distance 1 of some map point of tile d; in every draw some tile owner receives 2 blocks from every source; the totals per owner differ strongly between owners. `block_first`: listed blocks stay inside the source's 4 blocks. `point_pos`: points of one leaf block lie in increasing order within an interval of length 1. `map_pos`: the map points of one tile lie within an interval of length at most 6.
All inputs are finite; a program needn't handle non-finite values.
Results may differ from a plain program's by a relative error of at most 0.003.
Values may be sent and summed in bfloat16 or wider, within the bound.
A program may use at most 128 MiB of HBM per device.

v0:
```python
import functools

import jax
import jax.numpy as jnp
from jax import lax
from jax.experimental import pallas as pl
from jax.experimental.pallas import tpu as pltpu
from jax.sharding import PartitionSpec as P

AMPLITUDE = 0.2
FAR = -1e6
PIECES = 4
TOGETHER = 4
f32 = jnp.float32
bf16 = jnp.bfloat16


def split(value):
    high = value.astype(bf16)
    return high, (value - high.astype(f32)).astype(bf16)


def mm(a, b):
    return jnp.dot(a, b, preferred_element_type=f32)


def mm3(a, b):
    return mm(a[0], b[0]) + mm(a[0], b[1]) + mm(a[1], b[0])


def kernel(
    n,
    leaf,
    res_ref,
    inv_ref,
    bl_hbm,
    br_hbm,
    pp_ref,
    mp_ref,
    prior_ref,
    first_ref,
    count_ref,
    out_hbm,
    map_ref,
    bl_ref,
    br_ref,
    xs,
    rth,
    rtl,
    lh,
    ll,
    gf,
    gs,
    gr,
    tf,
    ts,
    tr,
    cbuf,
    co,
    mpb,
    wts,
    acc,
    ms,
    mr,
    fs,
    fr,
    ss,
    sr,
    lt,
    lr,
    send_sem,
    recv_sem,
    load_sem,
    store_sem,
):
    rows, samples = res_ref.shape
    rank = bl_ref.shape[2]
    levels = bl_ref.shape[0]
    half = samples // 2
    depth = n.bit_length() - 1
    tile = prior_ref.shape[0]
    me = lax.axis_index("pts")
    bits = [lax.rem(me // 2**k, 2) for k in range(depth)]
    partners = [me + 2**k * (1 - 2 * bits[k]) for k in range(depth)]
    par = bits[0]
    started = []

    def remote(src, dst, k):
        index = len(started)
        copy = pltpu.make_async_remote_copy(
            src_ref=src,
            dst_ref=dst,
            send_sem=send_sem.at[index],
            recv_sem=recv_sem.at[index],
            device_id={"pts": partners[k]},
            device_id_type=pl.DeviceIdType.MESH,
        )
        copy.start()
        started.append(copy)
        return copy

    order = list(range(depth)) + list(range(levels - 1, depth - 1, -1))
    loads = {}
    for l in order:
        for side, (src, dst) in enumerate(((br_hbm, br_ref), (bl_hbm, bl_ref))):
            loads[side, l] = pltpu.make_async_copy(
                src.at[l], dst.at[l], load_sem.at[side * levels + l]
            )
            loads[side, l].start()

    barrier = pltpu.get_barrier_semaphore()
    for k in range(depth):
        pl.semaphore_signal(
            barrier, inc=1, device_id={"pts": partners[k]}, device_id_type=pl.DeviceIdType.MESH
        )

    pairs = [m * (m + 1) // 2 for m in range(depth)]
    g_off, t_off = [], []
    g_at = t_at = 0
    for k in range(depth):
        m = depth - 1 - k
        g_off.append(g_at)
        t_off.append(t_at)
        g_at += pairs[m]
        t_at += m + 1

    mpb[0] = jnp.zeros((1, 128), f32)
    mpb[0, :, :tile] = mp_ref[0]
    for l in range(depth):
        loads[0, l].wait()
        loads[1, l].wait()
        high, low = split(br_ref[l].T)
        rth[l * rank : (l + 1) * rank, :] = high
        rtl[l * rank : (l + 1) * rank, :] = low
        high, low = split(bl_ref[l])
        lh[:, l * rank : (l + 1) * rank] = high
        ll[:, l * rank : (l + 1) * rank] = low
    at = 0
    for m in range(depth - 1, 0, -1):
        product = mm(rth[: m * rank, :], lh[:, m * rank : (m + 1) * rank])
        product = product.reshape(m, rank, rank)
        gf[at : at + m] = product
        gs[at : at + m] = product.astype(bf16)
        at += m

    pl.semaphore_wait(barrier, depth)

    def start_g(k):
        m = depth - 1 - k
        rest = pairs[m] - m
        copies = []
        if rest > 0:
            view = pl.ds(g_off[k] + m, rest)
            copies.append(remote(gs.at[view], gr.at[view], k))
        view = pl.ds(g_off[k], m)
        copies.append(remote(gs.at[view], gr.at[view], k))
        return copies

    def start_mp(k):
        return remote(mpb.at[pl.ds(0, 2**k)], mpb.at[pl.ds(2**k, 2**k)], k)

    g_heads = {0: start_g(0)} if depth > 1 else {}
    mp_copy = start_mp(0)

    def next_g(k):
        m = depth - 1 - k
        rest = pairs[m] - m
        if rest <= 0:
            return None
        g_heads[k][0].wait_recv()
        total = gf[g_off[k] + m : g_off[k] + pairs[m]] + gr[
            g_off[k] + m : g_off[k] + pairs[m]
        ].astype(f32)
        gf[g_off[k + 1] : g_off[k + 1] + rest] = total
        gs[g_off[k + 1] : g_off[k + 1] + rest] = total.astype(bf16)
        g_heads[k + 1] = start_g(k + 1)
        return None

    for b in range(rows // leaf):
        part = mm(inv_ref[b * leaf : (b + 1) * leaf, :], res_ref[b * leaf : (b + 1) * leaf, :])
        xs[b * leaf : (b + 1) * leaf, :] = part
    total_rows = rows * n
    for level in range(levels - 1, depth - 1, -1):
        loads[0, level].wait()
        loads[1, level].wait()
    for level in range(levels - 1, depth - 1, -1):
        size = total_rows // 2 ** (level + 1)
        count = rows // size
        projected = []
        for a in range(count):
            view = slice(a * size, (a + 1) * size)
            projected.append(split(mm3(split(br_ref[level, view, :].T), split(xs[view, :]))))
        for a in range(count):
            view = slice(a * size, (a + 1) * size)
            xs[view, :] += mm3(split(bl_ref[level, view, :]), projected[a ^ 1])

    if depth > 1:
        next_g(0)
    mp_copy.wait_recv()
    mp_next = 1
    if mp_next < depth:
        mp_copy = start_mp(mp_next)

    x_high, x_low = split(xs[...])
    t_all = mm(rth[...], x_high) + mm(rth[...], x_low) + mm(rtl[...], x_high)
    for h in range(2):
        t_half = t_all[:, h * half : (h + 1) * half].reshape(depth, rank, half)
        tf[h] = t_half
        ts[h, pl.ds(0, depth)] = t_half.astype(bf16)

    own_u = pp_ref[me]

    def weights(low_e, high_e):
        def one(e):
            spot = 0
            other = 0
            for i in range(depth):
                bit = lax.rem(e // 2**i, 2)
                spot = spot + bit * 2 ** (depth - 1 - i)
                other = other + lax.rem(bit + bits[i], 2) * 2**i
            first = first_ref[other, me]
            last = first + count_ref[other, me]
            t_col = jnp.broadcast_to(mpb[e], (128, 128)).T[:tile]
            base = pl.multiple_of(spot * tile, tile)
            for b in range(rows // leaf):
                u_row = own_u[:, b * leaf : (b + 1) * leaf]
                listed = jnp.logical_and(first <= b, b < last)
                u_row = jnp.where(listed, u_row, FAR)
                scaled = jnp.minimum(jnp.abs(t_col - u_row) * (2.0 * leaf), 1.0)
                rest = 1.0 - scaled
                square = rest * rest
                value = AMPLITUDE * (square * square * (1.0 + 4.0 * scaled))
                wts[pl.ds(base, tile), b * leaf : (b + 1) * leaf] = value.astype(bf16)

        def several(i, carry):
            for j in range(TOGETHER):
                one(low_e + i * TOGETHER + j)
            return carry

        lax.fori_loop(0, (high_e - low_e) // TOGETHER, several, 0)

    forwards = []
    for k in range(depth):
        m = depth - 1 - k
        span = pl.ds(t_off[k], m + 1)
        if k == 0:
            t_copies = [
                remote(ts.at[1 - par, span], tr.at[span], 0),
                remote(ts.at[par, m], cbuf.at[m, par], 0),
            ]
        else:
            t_copies = [remote(ts.at[par, span], tr.at[span], k)]
        if mp_next < depth:
            mp_copy.wait_recv()
            mp_next += 1
            if mp_next < depth:
                mp_copy = start_mp(mp_next)
        if k > 0 and m > 0:
            next_g(k)
        if k == depth - 2:
            while mp_next < depth:
                mp_copy.wait_recv()
                mp_next += 1
                if mp_next < depth:
                    mp_copy = start_mp(mp_next)
        late = k - (depth - 4)
        if late >= 0:
            weights(late * (n // 4), (late + 1) * (n // 4))
        for copy in t_copies:
            copy.wait_recv()
        if k > 0:
            forwards.append(remote(tr.at[t_off[k] + m], cbuf.at[m, par], 0))
        if m > 0:
            g_heads[k][-1].wait_recv()
            mine = ts[par, t_off[k] + m]
            theirs = tr[t_off[k] + m]
            g_mine = gs[g_off[k] : g_off[k] + m].reshape(m * rank, rank)
            g_theirs = gr[g_off[k] : g_off[k] + m].reshape(m * rank, rank)
            gained = mm(g_mine, theirs) + mm(g_theirs, mine)
            total = (
                tf[par, :m]
                + tr[t_off[k] : t_off[k] + m].astype(f32)
                + gained.reshape(m, rank, half)
            )
            tf[par, pl.ds(0, m)] = total
            ts[par, pl.ds(t_off[k + 1], m)] = total.astype(bf16)

    mine_cols = pl.ds(pl.multiple_of(par * half, half), half)
    other_cols = pl.ds(pl.multiple_of((1 - par) * half, half), half)

    def finish(columns, parts):
        stacked = jnp.concatenate(parts, axis=0)
        total = xs[:, columns] + mm(lh[...], stacked) + mm(ll[...], stacked)
        xs[:, columns] = total
        co[:, columns] = total.astype(bf16)

    finish(mine_cols, [tr[t_off[depth - 1 - m] + m] for m in range(depth)])
    for copy in forwards:
        copy.wait_recv()
    finish(other_cols, [cbuf[m, 1 - par] for m in range(depth)])

    store = pltpu.make_async_copy(xs, out_hbm, store_sem.at[0])
    store.start()

    quarter = n // 8 * tile
    half_rows = 4 * quarter
    first_copies = {}
    for j in (3, 2, 1, 0):
        low = half_rows + j * quarter
        ms[j] = mm(wts[low : low + quarter, :], co[...]).astype(bf16)
        first_copies[j] = remote(ms.at[j], mr.at[j], 0)

    def keep(j):
        part = mm(wts[j * quarter : (j + 1) * quarter, :], co[...])
        for c in range(2):
            acc[c, j] = part[:, c * half : (c + 1) * half]

    def summed(c, j):
        return acc[c, j] + mr[j, :, c * half : (c + 1) * half].astype(f32)

    keep(3)
    keep(2)
    first_copies[3].wait_recv()
    first_copies[2].wait_recv()
    fs[0, 0] = summed(0, 2).astype(bf16)
    fs[0, 1] = summed(0, 3).astype(bf16)
    copy_a = remote(fs.at[0], fr.at[0], 1)
    keep(1)
    first_copies[1].wait_recv()
    fs[1, 0] = summed(1, 1).astype(bf16)
    fs[1, 1] = summed(1, 3).astype(bf16)
    copy_b = remote(fs.at[1], fr.at[1], 2)
    keep(0)
    first_copies[0].wait_recv()
    acc[0, 1] = summed(0, 1)
    acc[1, 2] = summed(1, 2)
    acc[0, 0] = summed(0, 0)
    acc[1, 0] = summed(1, 0)
    copy_a.wait_recv()
    ss[0] = (acc[0, 1] + fr[0, 1].astype(f32)).astype(bf16)
    copy_a = remote(ss.at[0], sr.at[0], 2)
    copy_b.wait_recv()
    ss[1] = (acc[1, 2] + fr[1, 1].astype(f32)).astype(bf16)
    copy_b = remote(ss.at[1], sr.at[1], 1)
    sums = [acc[c, 0] + fr[c, 0].astype(f32) for c in range(2)]
    copy_a.wait_recv()
    copy_b.wait_recv()
    size = quarter
    for c in range(2):
        acc[c, 0] = sums[c] + sr[c].astype(f32)
    base = 0
    for k in range(3, depth):
        size = size // 2
        for c in range(2):
            lt[c, base : base + size, :] = acc[c, 0, size : 2 * size, :].astype(bf16)
        copy = remote(
            lt.at[:, pl.ds(base, size)], lr.at[:, pl.ds(base, size)], k
        )
        copy.wait_recv()
        for c in range(2):
            acc[c, 0, :size, :] += lr[c, base : base + size, :].astype(f32)
        base += size
    for c in range(2):
        cols = slice(c * half, (c + 1) * half)
        map_ref[:, cols] = prior_ref[:, cols].astype(f32) + acc[c, 0, :tile, :]
    store.wait()
    for copy in started:
        copy.wait_send()


def deliver(solved_ref, mapped_ref, out_ref, map_ref, held, spots, in_sem, out_sem):
    piece = held.shape[0] // PIECES
    moves = [(mapped_ref, spots, map_ref)]
    for i in range(PIECES):
        view = pl.ds(i * piece, piece)
        moves.append((solved_ref.at[view], held.at[view], out_ref.at[view]))
    reads = [pltpu.make_async_copy(a, b, in_sem.at[i]) for i, (a, b, _) in enumerate(moves)]
    writes = [pltpu.make_async_copy(b, c, out_sem.at[i]) for i, (_, b, c) in enumerate(moves)]
    for read in reads:
        read.start()
    for read, write in zip(reads, writes):
        read.wait()
        write.start()
    for write in writes:
        write.wait()


def body(
    residual_cols,
    leaf_inverse,
    basis_left,
    basis_right,
    point_pos,
    map_pos,
    prior_map,
    block_first,
    block_count,
):
    rows, samples = residual_cols.shape
    leaf = leaf_inverse.shape[1]
    levels, _, rank = basis_left.shape
    n = lax.axis_size("pts")
    depth = n.bit_length() - 1
    tile = map_pos.shape[0]
    half = samples // 2
    pair_total = sum(m * (m + 1) // 2 for m in range(depth))
    t_total = depth * (depth + 1) // 2
    vmem = pl.BlockSpec(memory_space=pltpu.VMEM)
    smem = pl.BlockSpec(memory_space=pltpu.SMEM)
    anywhere = pl.BlockSpec(memory_space=pl.ANY)
    copies = 6 * depth + 8
    quarter = n // 8 * tile
    solved, mapped = pl.pallas_call(
        functools.partial(kernel, n, leaf),
        out_shape=(
            jax.ShapeDtypeStruct((rows, samples), f32),
            jax.ShapeDtypeStruct((tile, samples), f32),
        ),
        in_specs=[vmem] * 2 + [anywhere] * 2 + [vmem] * 3 + [smem] * 2,
        out_specs=(anywhere, vmem),
        scratch_shapes=[
            pltpu.VMEM((levels, rows, rank), f32),
            pltpu.VMEM((levels, rows, rank), f32),
            pltpu.VMEM((rows, samples), f32),
            pltpu.VMEM((depth * rank, rows), bf16),
            pltpu.VMEM((depth * rank, rows), bf16),
            pltpu.VMEM((rows, depth * rank), bf16),
            pltpu.VMEM((rows, depth * rank), bf16),
            pltpu.VMEM((pair_total, rank, rank), f32),
            pltpu.VMEM((pair_total, rank, rank), bf16),
            pltpu.VMEM((pair_total, rank, rank), bf16),
            pltpu.VMEM((2, depth, rank, half), f32),
            pltpu.VMEM((2, t_total, rank, half), bf16),
            pltpu.VMEM((t_total, rank, half), bf16),
            pltpu.VMEM((depth, 2, rank, half), bf16),
            pltpu.VMEM((rows, samples), bf16),
            pltpu.VMEM((n, 1, 128), f32),
            pltpu.VMEM((n * tile, rows), bf16),
            pltpu.VMEM((2, 4, quarter, half), f32),
            pltpu.VMEM((4, quarter, samples), bf16),
            pltpu.VMEM((4, quarter, samples), bf16),
            pltpu.VMEM((2, 2, quarter, half), bf16),
            pltpu.VMEM((2, 2, quarter, half), bf16),
            pltpu.VMEM((2, quarter, half), bf16),
            pltpu.VMEM((2, quarter, half), bf16),
            pltpu.VMEM((2, quarter, half), bf16),
            pltpu.VMEM((2, quarter, half), bf16),
            pltpu.SemaphoreType.DMA((copies,)),
            pltpu.SemaphoreType.DMA((copies,)),
            pltpu.SemaphoreType.DMA((2 * levels,)),
            pltpu.SemaphoreType.DMA((1,)),
        ],
        compiler_params=pltpu.CompilerParams(
            collective_id=0, has_side_effects=True, vmem_limit_bytes=60 * 1024 * 1024
        ),
    )(
        residual_cols,
        leaf_inverse,
        basis_left,
        basis_right,
        point_pos.reshape(n, 1, rows),
        map_pos.reshape(1, 1, tile),
        prior_map,
        block_first,
        block_count,
    )
    return pl.pallas_call(
        deliver,
        out_shape=(
            jax.ShapeDtypeStruct((rows, samples), f32),
            jax.ShapeDtypeStruct((tile, samples), f32),
        ),
        in_specs=[anywhere] * 2,
        out_specs=(anywhere, anywhere),
        scratch_shapes=[
            pltpu.VMEM((rows, samples), f32),
            pltpu.VMEM((tile, samples), f32),
            pltpu.SemaphoreType.DMA((PIECES + 1,)),
            pltpu.SemaphoreType.DMA((PIECES + 1,)),
        ],
    )(solved, mapped)


def solution(mesh):
    in_specs = (
        P(("groups", "pts"), None),
        P(("groups", "pts"), None),
        P(None, ("groups", "pts"), None),
        P(None, ("groups", "pts"), None),
        P(),
        P("pts"),
        P(("groups", "pts"), None),
        P(),
        P(),
    )
    out_specs = (P(("groups", "pts"), None), P(("groups", "pts"), None))
    return jax.shard_map(body, mesh=mesh, in_specs=in_specs, out_specs=out_specs, check_vma=False)
```

profile of v0, /device:TPU:0, one launch (start us, length us, event | category | flops | bytes accessed | tf_op | source)
XLA Modules:
  0.0 51.1 jit_solution(9745763483166147892)
XLA Ops:
  0.6 48.6 %shard_map.104 = (f32[512,256]{1,0:T(8,128)}, f32[64,256]{1,0:T(8,128)}) custom-call(bf16[512,256]{1,0:T(8,128)(2,1)} %res_ref.1, bf16[512,128]{1,0:T(8,128)(2,1)} %inv_ref.1, f32[7,512,128]{2,1,0:T(8,128)} %bl_hbm.1, f32[7,512,128]{2,1,0:T(8,128)} %br_hbm.1, f32[32,1,512]{2,1,0:T(1,128)} %bitcast.2, f32[1,1,64]{2,1,0:T(1,128)} %bitcast.3, ...), custom_call_target="tpu_custom_call" | custom-call | tf_op jit(solution)/shard_map/pallas_call | solution.py:413
  49.2 1.9 %shard_map.105 = (f32[512,256]{1,0:T(8,128)}, f32[64,256]{1,0:T(8,128)}) custom-call(f32[512,256]{1,0:T(8,128)} %get-tuple-element.4.solved_ref, f32[64,256]{1,0:T(8,128)} %get-tuple-element.5.mapped_ref), custom_call_target="tpu_custom_call" | custom-call | tf_op jit(solution)/shard_map/pallas_call | solution.py:467
where the time goes:
time: 51.3 us; the launch traced here: 51.1 us
  Pallas kernels  50.4 us (98%)
  between operations  0.64 us (1%)
    pallas_call x1, Pallas kernels, body(): pl.pallas_call(functools.partial(kernel, n, leaf), out_shape=(jax.ShapeDt...  48.6 us
    pallas_call x1, Pallas kernels, body(): pl.pallas_call(deliver, out_shape=(jax.ShapeDtypeStruct((rows, samples),...  1.87 us

commit v1 on v0

v1 whole, which is shorter than its diff:
```python
import functools

import jax
import jax.numpy as jnp
from jax import lax
from jax.experimental import pallas as pl
from jax.experimental.pallas import tpu as pltpu
from jax.sharding import PartitionSpec as P

AMPLITUDE = 0.2
FAR = -1e6
PIECES = 4
TOGETHER = 4
SPLIT = (1,)
SENDS = 17
f32 = jnp.float32
bf16 = jnp.bfloat16


def mm(a, b):
    return jnp.dot(a, b, preferred_element_type=f32)


def kernel(
    n,
    leaf,
    res_hbm,
    inv_hbm,
    bl_hbm,
    br_hbm,
    pp_hbm,
    mp_hbm,
    prior_hbm,
    first_hbm,
    count_hbm,
    out_hbm,
    map_ref,
    res_ref,
    inv_ref,
    bl_ref,
    br_ref,
    pu,
    mp_ref,
    prior_ref,
    first_ref,
    count_ref,
    xs,
    rth,
    lh,
    gf,
    gs,
    gr,
    tf,
    ts,
    tr,
    cbuf,
    co,
    ps,
    mpb,
    wts,
    acc,
    ms,
    mr,
    fs,
    fr,
    ss,
    sr,
    lt,
    lr,
    zs,
    zr,
    send_sem,
    recv_sem,
    load_sem,
    store_sem,
):
    rows, samples = res_ref.shape
    rank = bl_ref.shape[2]
    levels = bl_ref.shape[0]
    half = samples // 2
    depth = n.bit_length() - 1
    tile = prior_ref.shape[0]
    late = samples // rank
    early = depth - late
    me = lax.axis_index("pts")
    bits = [lax.rem(me // 2**k, 2) for k in range(depth)]
    par = bits[0]
    pool = [None] * send_sem.shape[0]
    arrivals = []
    sends = []

    def partner(mask):
        device = me
        for k in range(depth):
            if (mask >> k) & 1:
                device = device + 2**k * (1 - 2 * bits[k])
        return device

    def describe(src, dst, send, recv, mask):
        return pltpu.make_async_remote_copy(
            src_ref=src,
            dst_ref=dst,
            send_sem=send_sem.at[send],
            recv_sem=recv_sem.at[recv],
            device_id={"pts": partner(mask)},
            device_id_type=pl.DeviceIdType.MESH,
        )

    def arrival():
        arrivals.append(len(arrivals))
        return arrivals[-1]

    def remote(src, dst, mask):
        slot = len(sends) % (len(pool) - 1) + 1
        if pool[slot] is not None:
            pool[slot].wait_send()
        copy = describe(src, dst, slot, arrival(), mask)
        copy.start()
        pool[slot] = copy
        sends.append(copy)
        return copy

    loads = {}

    def load(name, src, dst):
        loads[name] = pltpu.make_async_copy(src, dst, load_sem.at[len(loads)])
        loads[name].start()

    tree = pl.ds(0, depth)
    load("r", br_hbm.at[tree], br_ref.at[tree])
    load("l", bl_hbm.at[tree], bl_ref.at[tree])
    load("inv", inv_hbm, inv_ref)
    load("res", res_hbm, res_ref)
    for l in range(levels - 1, depth - 1, -1):
        load(("r", l), br_hbm.at[l], br_ref.at[l])
        load(("l", l), bl_hbm.at[l], bl_ref.at[l])

    barrier = pltpu.get_barrier_semaphore()
    for mask in range(1, n):
        pl.semaphore_signal(
            barrier, inc=1, device_id={"pts": partner(mask)}, device_id_type=pl.DeviceIdType.MESH
        )
    load("mp", mp_hbm, mp_ref)
    load("pp", pp_hbm.at[me], pu)
    load("first", first_hbm, first_ref)
    load("count", count_hbm, count_ref)
    load("prior", prior_hbm, prior_ref)

    pairs = [m * (m + 1) // 2 for m in range(depth)]
    g_off, t_off = [], []
    g_at = t_at = 0
    for k in range(depth):
        m = depth - 1 - k
        g_off.append(g_at)
        t_off.append(t_at)
        g_at += pairs[m]
        t_at += m + 1

    loads["r"].wait()
    for l in range(depth - 1, -1, -1):
        rth[l * rank : (l + 1) * rank, :] = br_ref[l].astype(bf16).T
    loads["l"].wait()
    for l in range(depth - 1, -1, -1):
        lh[:, l * rank : (l + 1) * rank] = bl_ref[l].astype(bf16)
    for m in range(depth - 1, 0, -2):
        low = max(m - 1, 1)
        product = mm(rth[: m * rank, :], lh[:, low * rank : (m + 1) * rank])
        for i in range(m, low - 1, -1):
            start = sum(range(i + 1, depth))
            part = product[: i * rank, (i - low) * rank : (i - low + 1) * rank]
            part = part.reshape(i, rank, rank)
            gf[start : start + i] = part
            gs[start : start + i] = part.astype(bf16)
    for name in ("mp", "pp", "first", "count", "prior"):
        loads[name].wait()
    mpb[0] = jnp.zeros((1, 128), f32)
    mpb[0, :, :tile] = mp_ref[0]

    with jax.named_scope("barrier"):
        pl.semaphore_wait(barrier, n - 1)

    group = 2**early
    spots = []
    for first_mask in range(0, n, group):
        low = max(first_mask, 1)
        recv = arrival()
        for mask in range(low, first_mask + group):
            describe(mpb.at[0], mpb.at[mask], 0, recv, mask).start()
        view = mpb.at[pl.ds(low, first_mask + group - low)]
        spots.append(describe(view, view, 0, recv, 1))
    others = mpb.at[pl.ds(1, n - 1)]
    pool[0] = describe(others, others, 0, 0, 1)

    g_copies = {}
    rank_half = rank // 2
    core_rows = pl.ds(pl.multiple_of(par * rank_half, rank_half), rank_half)

    def g_span(k, part):
        m = depth - 1 - k
        if part == "head":
            return g_off[k], m
        return g_off[k] + m, pairs[m] - m

    def g_send(k, part):
        start, size = g_span(k, part)
        if size == 0:
            return
        span = pl.ds(start, size)
        if k in SPLIT:
            copy = remote(gs.at[span, core_rows], gr.at[span, core_rows], 2**k)
        else:
            copy = remote(gs.at[span], gr.at[span], 2**k)
        g_copies[k, part] = copy

    def g_relay(k, part):
        start, size = g_span(k, part)
        if k not in SPLIT or size == 0:
            return
        g_copies[k, part].wait_recv()
        view = gr.at[pl.ds(start, size), core_rows]
        g_copies[k, part] = remote(view, view, 1)

    def g_wait(k, part):
        if (k, part) in g_copies:
            g_copies.pop((k, part)).wait_recv()

    def g_next(k):
        start, size = g_span(k, "rest")
        if size == 0:
            return
        g_wait(k, "rest")
        total = gf[start : start + size] + gr[start : start + size].astype(f32)
        gf[g_off[k + 1] : g_off[k + 1] + size] = total
        gs[g_off[k + 1] : g_off[k + 1] + size] = total.astype(bf16)

    g_send(0, "rest")
    g_send(0, "head")

    loads["inv"].wait()
    loads["res"].wait()
    for b in range(rows // leaf):
        view = slice(b * leaf, (b + 1) * leaf)
        xs[view, :] = mm(inv_ref[view, :], res_ref[view, :])
    total_rows = rows * n
    for level in range(levels - 1, depth - 1, -1):
        loads["r", level].wait()
        loads["l", level].wait()
        size = total_rows // 2 ** (level + 1)
        count = rows // size
        projected = []
        for a in range(count):
            view = slice(a * size, (a + 1) * size)
            part = mm(br_ref[level, view, :].astype(bf16).T, xs[view, :].astype(bf16))
            projected.append(part.astype(bf16))
        for a in range(count):
            view = slice(a * size, (a + 1) * size)
            xs[view, :] += mm(bl_ref[level, view, :].astype(bf16), projected[a ^ 1])
    t_all = mm(rth[...], xs[...].astype(bf16))
    for h in range(2):
        t_half = t_all[:, h * half : (h + 1) * half].reshape(depth, rank, half)
        tf[h] = t_half
        ts[h, pl.ds(0, depth)] = t_half.astype(bf16)

    top = depth - 1
    t_copies = {
        (0, "urgent"): [
            remote(ts.at[1 - par, pl.ds(late, depth - late)], tr.at[pl.ds(late, depth - late)], 1),
            remote(ts.at[par, top], cbuf.at[top, par], 1),
        ],
        (0, "rest"): [remote(ts.at[1 - par, pl.ds(0, late)], tr.at[pl.ds(0, late)], 1)],
    }

    def combine(k, low, high):
        m = depth - 1 - k
        if high <= low:
            return
        count = high - low
        mine = ts[par, t_off[k] + m]
        theirs = tr[t_off[k] + m]
        g_mine = gs[g_off[k] + low : g_off[k] + high].reshape(count * rank, rank)
        g_theirs = gr[g_off[k] + low : g_off[k] + high].reshape(count * rank, rank)
        gained = mm(g_mine, theirs) + mm(g_theirs, mine)
        total = (
            tf[par, low:high]
            + tr[t_off[k] + low : t_off[k] + high].astype(f32)
            + gained.reshape(count, rank, half)
        )
        tf[par, low:high] = total
        ts[par, t_off[k + 1] + low : t_off[k + 1] + high] = total.astype(bf16)

    def t_send(k, low, high, name):
        span = pl.ds(t_off[k] + low, high - low)
        t_copies[k, name] = [remote(ts.at[par, span], tr.at[span], 2**k)]

    def t_wait(k, name):
        for copy in t_copies.pop((k, name), []):
            copy.wait_recv()

    forwards = {}

    def forward(k):
        m = depth - 1 - k
        forwards[m] = remote(tr.at[t_off[k] + m], cbuf.at[m, par], 1)

    def weights(low_e, high_e):
        with jax.named_scope(f"spot{low_e}"):
            spots[low_e // group].wait_recv()
        own_u = pu[...]

        def one(e):
            spot = 0
            other = 0
            for i in range(depth):
                bit = lax.rem(e // 2**i, 2)
                spot = spot + bit * 2 ** (depth - 1 - i)
                other = other + lax.rem(bit + bits[i], 2) * 2**i
            first = first_ref[other, me]
            last = first + count_ref[other, me]
            t_col = jnp.broadcast_to(mpb[e], (128, 128)).T[:tile]
            base = pl.multiple_of(spot * tile, tile)
            for b in range(rows // leaf):
                u_row = own_u[:, b * leaf : (b + 1) * leaf]
                listed = jnp.logical_and(first <= b, b < last)
                u_row = jnp.where(listed, u_row, FAR)
                scaled = jnp.minimum(jnp.abs(t_col - u_row) * (2.0 * leaf), 1.0)
                rest = 1.0 - scaled
                square = rest * rest
                value = AMPLITUDE * (square * square * (1.0 + 4.0 * scaled))
                wts[pl.ds(base, tile), b * leaf : (b + 1) * leaf] = value.astype(bf16)

        def several(i, carry):
            for j in range(TOGETHER):
                one(low_e + i * TOGETHER + j)
            return carry

        lax.fori_loop(0, (high_e - low_e) // TOGETHER, several, 0)

    quarter = n // 8 * tile
    half_rows = 4 * quarter
    sums = {}

    def map_first(s, factor, order):
        for j in order:
            low = half_rows + j * quarter
            ms[s, j] = mm(wts[low : low + quarter, :], factor[...]).astype(bf16)
            sums[s, j] = remote(ms.at[s, j], mr.at[s, j], 1)

    def keep(s, j, factor):
        part = mm(wts[j * quarter : (j + 1) * quarter, :], factor[...])
        with jax.named_scope(f"first{s}{j}"):
            sums[s, j].wait_recv()
        part = part + mr[s, j].astype(f32)
        return [part[:, c * half : (c + 1) * half] for c in range(2)]

    def map_second(s, factor):
        def to_x(slot, value):
            fs[s, 0, slot] = value.astype(bf16)
            sums[s, "x", slot] = remote(fs.at[s, 0, slot], fr.at[s, 0, slot], 2)

        def to_y(slot, value):
            fs[s, 1, slot] = value.astype(bf16)
            sums[s, "y", slot] = remote(fs.at[s, 1, slot], fr.at[s, 1, slot], 4)

        part = keep(s, 3, factor)
        to_x(1, part[0])
        to_y(1, part[1])
        part = keep(s, 2, factor)
        to_x(0, part[0])
        acc[s, 1, 1] = part[1]
        part = keep(s, 1, factor)
        to_y(0, part[1])
        acc[s, 0, 1] = part[0]
        part = keep(s, 0, factor)
        acc[s, 0, 0] = part[0]
        acc[s, 1, 0] = part[1]

    def map_third(s):
        with jax.named_scope(f"third{s}"):
            sums[s, "x", 1].wait_recv()
        ss[s, 0] = (acc[s, 0, 1] + fr[s, 0, 1].astype(f32)).astype(bf16)
        sums[s, "xy"] = remote(ss.at[s, 0], sr.at[s, 0], 4)
        with jax.named_scope(f"thirdb{s}"):
            sums[s, "y", 1].wait_recv()
        ss[s, 1] = (acc[s, 1, 1] + fr[s, 1, 1].astype(f32)).astype(bf16)
        sums[s, "yx"] = remote(ss.at[s, 1], sr.at[s, 1], 2)

    def map_fourth(s):
        with jax.named_scope(f"fourth{s}"):
            for name in ((s, "x", 0), (s, "y", 0), (s, "xy"), (s, "yx")):
                sums[name].wait_recv()
        size = quarter
        for c in range(2):
            acc[s, c, 0] += fr[s, c, 0].astype(f32) + sr[s, c].astype(f32)
        base = 0
        for k in range(3, early):
            size = size // 2
            for c in range(2):
                lt[s, c, base : base + size, :] = acc[s, c, 0, size : 2 * size, :].astype(bf16)
            view = pl.ds(base, size)
            copy = remote(lt.at[s, :, view], lr.at[s, :, view], 2**k)
            copy.wait_recv()
            for c in range(2):
                acc[s, c, 0, :size, :] += lr[s, c, base : base + size, :].astype(f32)
            base += size
        return jnp.concatenate([acc[s, c, 0, :size, :] for c in range(2)], axis=1)

    late_factor = lh.at[:, pl.ds(0, late * rank)]

    def urgent(k):
        m = depth - 1 - k
        with jax.named_scope(f"turgent{k}"):
            t_wait(k, "urgent")
        if k > 0:
            forward(k)
        if m > late:
            with jax.named_scope(f"ghead{k}"):
                g_wait(k, "head")
            combine(k, late, m)
            t_send(k + 1, late, m, "urgent")

    def rest(k):
        with jax.named_scope(f"trest{k}"):
            t_wait(k, "rest")
        with jax.named_scope(f"gheadb{k}"):
            g_wait(k, "head")
        combine(k, 0, min(late, depth - 1 - k))
        t_send(k + 1, 0, min(late, depth - 1 - k), "rest")

    def factors(k):
        with jax.named_scope(f"gnext{k}"):
            g_next(k)
        g_send(k + 1, "head")
        g_send(k + 1, "rest")

    with jax.named_scope("gnext0"):
        g_next(0)
    g_send(1, "head")
    urgent(0)
    g_send(1, "rest")
    rest(0)
    for i in range(n // group):
        weights(i * group, (i + 1) * group)
        if i == 1:
            with jax.named_scope("relay0"):
                g_relay(1, "head")
    for k in range(1, early):
        if k > 1 and depth - 1 - k > late:
            factors(k - 1)
        urgent(k)
        if k == 1:
            map_first(0, late_factor, (3, 2))
            with jax.named_scope("relay1"):
                g_relay(1, "rest")
            map_first(0, late_factor, (1, 0))
        else:
            if depth - 1 - k <= late:
                factors(k - 1)
            rest(k - 1)
    map_second(0, late_factor)

    mine_cols = pl.ds(pl.multiple_of(par * half, half), half)
    other_cols = pl.ds(pl.multiple_of((1 - par) * half, half), half)

    def own(m):
        return tr[t_off[depth - 1 - m] + m]

    def sibling(m):
        return cbuf[m, 1 - par]

    def finish(columns, parts):
        stacked = jnp.concatenate(parts, axis=0)
        ps[late * rank :, columns] = stacked
        co[:, columns] = (xs[:, columns] + mm(lh[:, late * rank :], stacked)).astype(bf16)

    finish(mine_cols, [own(m) for m in range(late, depth)])
    with jax.named_scope("forwards"):
        for m in range(late, depth - 1):
            forwards[m].wait_recv()
    finish(other_cols, [sibling(m) for m in range(late, depth)])
    map_first(1, co, (3, 2, 1, 0))
    rest(early - 1)
    factors(early - 1)
    map_third(0)
    map_second(1, co)
    for k in range(early, depth):
        with jax.named_scope(f"turgent{k}"):
            t_wait(k, "rest")
        forward(k)
        if k < depth - 1:
            rest(k)
            factors(k)
        if k == early:
            map_third(1)
            corrections = map_fourth(0).astype(bf16)
            partial = map_fourth(1)
    for m in range(late):
        ps[m * rank : (m + 1) * rank, mine_cols] = own(m)
    with jax.named_scope("forwards2"):
        for m in range(late):
            forwards[m].wait_recv()
    for m in range(late):
        ps[m * rank : (m + 1) * rank, other_cols] = sibling(m)
    total = partial + mm(corrections, ps[: late * rank])
    lines = []
    for v in (3, 1, 2):
        mask = 0
        for i in range(late):
            mask += ((v >> (late - 1 - i)) & 1) * 2 ** (early + i)
        zs[v] = total[v * tile : (v + 1) * tile].astype(bf16)
        lines.append((v, remote(zs.at[v], zr.at[v], mask)))
    xs[...] += mm(lh[...], ps[...])
    for l in range(depth):
        view = slice(l * rank, (l + 1) * rank)
        low = (bl_ref[l] - lh[:, view].astype(f32)).astype(bf16)
        xs[...] += mm(low, ps[view, :])
    store = pltpu.make_async_copy(xs, out_hbm, store_sem.at[0])
    store.start()
    result = prior_ref[...].astype(f32) + total[:tile]
    for v, copy in lines:
        with jax.named_scope(f"line{v}"):
            copy.wait_recv()
        result = result + zr[v].astype(f32)
    map_ref[...] = result
    with jax.named_scope("end"):
        store.wait()
        for copy in pool:
            copy.wait_send()
    assert len(arrivals) == recv_sem.shape[0], len(arrivals)


def deliver(solved_ref, mapped_ref, out_ref, map_ref, held, spots, in_sem, out_sem):
    piece = held.shape[0] // PIECES
    moves = [(mapped_ref, spots, map_ref)]
    for i in range(PIECES):
        view = pl.ds(i * piece, piece)
        moves.append((solved_ref.at[view], held.at[view], out_ref.at[view]))
    reads = [pltpu.make_async_copy(a, b, in_sem.at[i]) for i, (a, b, _) in enumerate(moves)]
    writes = [pltpu.make_async_copy(b, c, out_sem.at[i]) for i, (_, b, c) in enumerate(moves)]
    for read in reads:
        read.start()
    for read, write in zip(reads, writes):
        read.wait()
        write.start()
    for write in writes:
        write.wait()


def body(
    residual_cols,
    leaf_inverse,
    basis_left,
    basis_right,
    point_pos,
    map_pos,
    prior_map,
    block_first,
    block_count,
):
    rows, samples = residual_cols.shape
    leaf = leaf_inverse.shape[1]
    levels, _, rank = basis_left.shape
    n = lax.axis_size("pts")
    depth = n.bit_length() - 1
    tile = map_pos.shape[0]
    half = samples // 2
    late = samples // rank
    pair_total = sum(m * (m + 1) // 2 for m in range(depth))
    t_total = depth * (depth + 1) // 2
    vmem = pl.BlockSpec(memory_space=pltpu.VMEM)
    anywhere = pl.BlockSpec(memory_space=pl.ANY)
    line = 2**late
    early = depth - late
    products = sum((2 if m > 1 else 1) * (2 if depth - 1 - m in SPLIT else 1) for m in range(1, depth))
    copies = line + 2 * early + late + depth + products + 2 * (early + 7) + line - 1
    quarter = n // 8 * tile
    solved, mapped = pl.pallas_call(
        functools.partial(kernel, n, leaf),
        out_shape=(
            jax.ShapeDtypeStruct((rows, samples), f32),
            jax.ShapeDtypeStruct((tile, samples), f32),
        ),
        in_specs=[anywhere] * 9,
        out_specs=(anywhere, vmem),
        scratch_shapes=[
            pltpu.VMEM((rows, samples), bf16),
            pltpu.VMEM((rows, leaf), bf16),
            pltpu.VMEM((levels, rows, rank), f32),
            pltpu.VMEM((levels, rows, rank), f32),
            pltpu.VMEM((1, rows), f32),
            pltpu.VMEM((1, 1, tile), f32),
            pltpu.VMEM((tile, samples), bf16),
            pltpu.SMEM((n, n), jnp.int32),
            pltpu.SMEM((n, n), jnp.int32),
            pltpu.VMEM((rows, samples), f32),
            pltpu.VMEM((depth * rank, rows), bf16),
            pltpu.VMEM((rows, depth * rank), bf16),
            pltpu.VMEM((pair_total, rank, rank), f32),
            pltpu.VMEM((pair_total, rank, rank), bf16),
            pltpu.VMEM((pair_total, rank, rank), bf16),
            pltpu.VMEM((2, depth, rank, half), f32),
            pltpu.VMEM((2, t_total, rank, half), bf16),
            pltpu.VMEM((t_total, rank, half), bf16),
            pltpu.VMEM((depth, 2, rank, half), bf16),
            pltpu.VMEM((rows, samples), bf16),
            pltpu.VMEM((depth * rank, samples), bf16),
            pltpu.VMEM((n, 1, 128), f32),
            pltpu.VMEM((n * tile, rows), bf16),
            pltpu.VMEM((2, 2, 2, quarter, half), f32),
            pltpu.VMEM((2, 4, quarter, samples), bf16),
            pltpu.VMEM((2, 4, quarter, samples), bf16),
            pltpu.VMEM((2, 2, 2, quarter, half), bf16),
            pltpu.VMEM((2, 2, 2, quarter, half), bf16),
            pltpu.VMEM((2, 2, quarter, half), bf16),
            pltpu.VMEM((2, 2, quarter, half), bf16),
            pltpu.VMEM((2, 2, quarter, half), bf16),
            pltpu.VMEM((2, 2, quarter, half), bf16),
            pltpu.VMEM((line, tile, samples), bf16),
            pltpu.VMEM((line, tile, samples), bf16),
            pltpu.SemaphoreType.DMA((SENDS,)),
            pltpu.SemaphoreType.DMA((copies,)),
            pltpu.SemaphoreType.DMA((2 * (levels - depth) + 9,)),
            pltpu.SemaphoreType.DMA((1,)),
        ],
        compiler_params=pltpu.CompilerParams(
            collective_id=0, has_side_effects=True, vmem_limit_bytes=60 * 1024 * 1024
        ),
    )(
        residual_cols,
        leaf_inverse,
        basis_left,
        basis_right,
        point_pos.reshape(n, 1, rows),
        map_pos.reshape(1, 1, tile),
        prior_map,
        block_first,
        block_count,
    )
    return pl.pallas_call(
        deliver,
        out_shape=(
            jax.ShapeDtypeStruct((rows, samples), f32),
            jax.ShapeDtypeStruct((tile, samples), f32),
        ),
        in_specs=[anywhere] * 2,
        out_specs=(anywhere, anywhere),
        scratch_shapes=[
            pltpu.VMEM((rows, samples), f32),
            pltpu.VMEM((tile, samples), f32),
            pltpu.SemaphoreType.DMA((PIECES + 1,)),
            pltpu.SemaphoreType.DMA((PIECES + 1,)),
        ],
    )(solved, mapped)


def solution(mesh):
    in_specs = (
        P(("groups", "pts"), None),
        P(("groups", "pts"), None),
        P(None, ("groups", "pts"), None),
        P(None, ("groups", "pts"), None),
        P(),
        P("pts"),
        P(("groups", "pts"), None),
        P(),
        P(),
    )
    out_specs = (P(("groups", "pts"), None), P(("groups", "pts"), None))
    return jax.shard_map(body, mesh=mesh, in_specs=in_specs, out_specs=out_specs, check_vma=False)
```

time: 51.3 us -> 40.6 us (0.79)
  Pallas kernels: 50.4 us -> 39.8 us
    pallas_call x1, Pallas kernels: 48.6 us -> 37.9 us  [body(): pl.pallas_call(functools.partial(kernel, n, leaf), out_shape=(jax.ShapeDt...]
where the time goes in v1:
time: 40.6 us; the launch traced here: 40.5 us
  Pallas kernels  39.8 us (98%)
  between operations  0.64 us (2%)
    pallas_call x1, Pallas kernels, body(): pl.pallas_call(functools.partial(kernel, n, leaf), out_shape=(jax.ShapeDt...  37.9 us
    pallas_call x1, Pallas kernels, body(): pl.pallas_call(deliver, out_shape=(jax.ShapeDtypeStruct((rows, samples),...  1.87 us

profile of v1, /device:TPU:0, one launch (start us, length us, event | category | flops | bytes accessed | tf_op | source)
XLA Modules:
  0.0 40.5 jit_solution(3988817075064797741)
XLA Ops:
  0.6 37.9 %shard_map.104 = (f32[512,256]{1,0:T(8,128)}, f32[64,256]{1,0:T(8,128)}) custom-call(bf16[512,256]{1,0:T(8,128)(2,1)} %res_hbm.1, bf16[512,128]{1,0:T(8,128)(2,1)} %inv_hbm.1, f32[7,512,128]{2,1,0:T(8,128)} %bl_hbm.1, f32[7,512,128]{2,1,0:T(8,128)} %br_hbm.1, f32[32,1,512]{2,1,0:T(1,128)} %bitcast.2, f32[1,1,64]{2,1,0:T(1,128)} %bitcast.3, ...), custom_call_target="tpu_custom_call" | custom-call | tf_op jit(solution)/shard_map/pallas_call | solution.py:576
  38.6 1.9 %shard_map.105 = (f32[512,256]{1,0:T(8,128)}, f32[64,256]{1,0:T(8,128)}) custom-call(f32[512,256]{1,0:T(8,128)} %get-tuple-element.4.solved_ref, f32[64,256]{1,0:T(8,128)} %get-tuple-element.5.mapped_ref), custom_call_target="tpu_custom_call" | custom-call | tf_op jit(solution)/shard_map/pallas_call | solution.py:638

commit v2 on v1

--- a/solution.py
+++ b/solution.py
@@ -13,6 +13,7 @@
 TOGETHER = 4
 SPLIT = (1,)
 SENDS = 17
+VMEM_LIMIT = 50 * 1024 * 1024
 f32 = jnp.float32
 bf16 = jnp.bfloat16
 
@@ -33,7 +34,7 @@
     prior_hbm,
     first_hbm,
     count_hbm,
-    out_hbm,
+    xs,
     map_ref,
     res_ref,
     inv_ref,
@@ -44,7 +45,6 @@
     prior_ref,
     first_ref,
     count_ref,
-    xs,
     rth,
     lh,
     gf,
@@ -72,7 +72,6 @@
     send_sem,
     recv_sem,
     load_sem,
-    store_sem,
 ):
     rows, samples = res_ref.shape
     rank = bl_ref.shape[2]
@@ -126,11 +125,11 @@
         loads[name] = pltpu.make_async_copy(src, dst, load_sem.at[len(loads)])
         loads[name].start()
 
+    load("inv", inv_hbm, inv_ref)
+    load("res", res_hbm, res_ref)
     tree = pl.ds(0, depth)
     load("r", br_hbm.at[tree], br_ref.at[tree])
     load("l", bl_hbm.at[tree], bl_ref.at[tree])
-    load("inv", inv_hbm, inv_ref)
-    load("res", res_hbm, res_ref)
     for l in range(levels - 1, depth - 1, -1):
         load(("r", l), br_hbm.at[l], br_ref.at[l])
         load(("l", l), bl_hbm.at[l], bl_ref.at[l])
@@ -156,6 +155,11 @@
         g_at += pairs[m]
         t_at += m + 1
 
+    loads["inv"].wait()
+    loads["res"].wait()
+    for b in range(rows // leaf):
+        view = slice(b * leaf, (b + 1) * leaf)
+        xs[view, :] = mm(inv_ref[view, :], res_ref[view, :])
     loads["r"].wait()
     for l in range(depth - 1, -1, -1):
         rth[l * rank : (l + 1) * rank, :] = br_ref[l].astype(bf16).T
@@ -192,6 +196,7 @@
     pool[0] = describe(others, others, 0, 0, 1)
 
     g_copies = {}
+    relayed = set()
     rank_half = rank // 2
     core_rows = pl.ds(pl.multiple_of(par * rank_half, rank_half), rank_half)
 
@@ -214,14 +219,16 @@
 
     def g_relay(k, part):
         start, size = g_span(k, part)
-        if k not in SPLIT or size == 0:
+        if k not in SPLIT or size == 0 or (k, part) in relayed:
             return
+        relayed.add((k, part))
         g_copies[k, part].wait_recv()
         view = gr.at[pl.ds(start, size), core_rows]
         g_copies[k, part] = remote(view, view, 1)
 
     def g_wait(k, part):
         if (k, part) in g_copies:
+            g_relay(k, part)
             g_copies.pop((k, part)).wait_recv()
 
     def g_next(k):
@@ -236,11 +243,6 @@
     g_send(0, "rest")
     g_send(0, "head")
 
-    loads["inv"].wait()
-    loads["res"].wait()
-    for b in range(rows // leaf):
-        view = slice(b * leaf, (b + 1) * leaf)
-        xs[view, :] = mm(inv_ref[view, :], res_ref[view, :])
     total_rows = rows * n
     for level in range(levels - 1, depth - 1, -1):
         loads["r", level].wait()
@@ -302,9 +304,11 @@
         m = depth - 1 - k
         forwards[m] = remote(tr.at[t_off[k] + m], cbuf.at[m, par], 1)
 
-    def weights(low_e, high_e):
-        with jax.named_scope(f"spot{low_e}"):
-            spots[low_e // group].wait_recv()
+    def weights(place, core):
+        if core == 1:
+            with jax.named_scope(f"spot{place}"):
+                spots[place].wait_recv()
+        start = place * group + core
         own_u = pu[...]
 
         def one(e):
@@ -330,10 +334,10 @@
 
         def several(i, carry):
             for j in range(TOGETHER):
-                one(low_e + i * TOGETHER + j)
+                one(start + 2 * (i * TOGETHER + j))
             return carry
 
-        lax.fori_loop(0, (high_e - low_e) // TOGETHER, several, 0)
+        lax.fori_loop(0, group // 2 // TOGETHER, several, 0)
 
     quarter = n // 8 * tile
     half_rows = 4 * quarter
@@ -352,57 +356,82 @@
         part = part + mr[s, j].astype(f32)
         return [part[:, c * half : (c + 1) * half] for c in range(2)]
 
-    def map_second(s, factor):
+    def late_second(order):
+        for j in order:
+            part = keep(0, j, late_factor)
+            for c in range(2):
+                if j > 1:
+                    fs[0, j - 2, c] = part[c].astype(bf16)
+                else:
+                    acc[0, j, c] = part[c]
+            if j == 3:
+                sums[0, "x", 1] = remote(fs.at[0, 1], fr.at[0, 1], 2)
+            if j == 2:
+                sums[0, "x", 0] = remote(fs.at[0, 0, 0], fr.at[0, 0, 0], 2)
+
+    def late_rest():
+        sums[0, "x", 2] = remote(fs.at[0, 0, 1], fr.at[0, 0, 1], 2)
+
+    def late_third():
+        with jax.named_scope("third0"):
+            sums[0, "x", 1].wait_recv()
+        ss[0] = (acc[0, 1] + fr[0, 1].astype(f32)).astype(bf16)
+        sums[0, "y"] = remote(ss.at[0], sr.at[0], 4)
+
+    def map_second(order):
         def to_x(slot, value):
-            fs[s, 0, slot] = value.astype(bf16)
-            sums[s, "x", slot] = remote(fs.at[s, 0, slot], fr.at[s, 0, slot], 2)
+            fs[1, slot, 0] = value.astype(bf16)
+            sums[1, "x", slot] = remote(fs.at[1, slot, 0], fr.at[1, slot, 0], 2)
 
         def to_y(slot, value):
-            fs[s, 1, slot] = value.astype(bf16)
-            sums[s, "y", slot] = remote(fs.at[s, 1, slot], fr.at[s, 1, slot], 4)
-
-        part = keep(s, 3, factor)
-        to_x(1, part[0])
-        to_y(1, part[1])
-        part = keep(s, 2, factor)
-        to_x(0, part[0])
-        acc[s, 1, 1] = part[1]
-        part = keep(s, 1, factor)
-        to_y(0, part[1])
-        acc[s, 0, 1] = part[0]
-        part = keep(s, 0, factor)
-        acc[s, 0, 0] = part[0]
-        acc[s, 1, 0] = part[1]
-
-    def map_third(s):
-        with jax.named_scope(f"third{s}"):
-            sums[s, "x", 1].wait_recv()
-        ss[s, 0] = (acc[s, 0, 1] + fr[s, 0, 1].astype(f32)).astype(bf16)
-        sums[s, "xy"] = remote(ss.at[s, 0], sr.at[s, 0], 4)
-        with jax.named_scope(f"thirdb{s}"):
-            sums[s, "y", 1].wait_recv()
-        ss[s, 1] = (acc[s, 1, 1] + fr[s, 1, 1].astype(f32)).astype(bf16)
-        sums[s, "yx"] = remote(ss.at[s, 1], sr.at[s, 1], 2)
+            fs[1, slot, 1] = value.astype(bf16)
+            sums[1, "y", slot] = remote(fs.at[1, slot, 1], fr.at[1, slot, 1], 4)
+
+        for j in order:
+            part = keep(1, j, co)
+            if j == 3:
+                to_x(1, part[0])
+                to_y(1, part[1])
+            if j == 2:
+                to_x(0, part[0])
+                acc[1, 1, 1] = part[1]
+            if j == 1:
+                to_y(0, part[1])
+                acc[1, 1, 0] = part[0]
+            if j == 0:
+                for c in range(2):
+                    acc[1, 0, c] = part[c]
+
+    def map_third():
+        with jax.named_scope("third1"):
+            sums[1, "x", 1].wait_recv()
+        ss[1, 0] = (acc[1, 1, 0] + fr[1, 1, 0].astype(f32)).astype(bf16)
+        sums[1, "xy"] = remote(ss.at[1, 0], sr.at[1, 0], 4)
+        with jax.named_scope("thirdb1"):
+            sums[1, "y", 1].wait_recv()
+        ss[1, 1] = (acc[1, 1, 1] + fr[1, 1, 1].astype(f32)).astype(bf16)
+        sums[1, "yx"] = remote(ss.at[1, 1], sr.at[1, 1], 2)
 
     def map_fourth(s):
         with jax.named_scope(f"fourth{s}"):
-            for name in ((s, "x", 0), (s, "y", 0), (s, "xy"), (s, "yx")):
-                sums[name].wait_recv()
+            for name in (("x", 0), ("x", 2), ("y", 0), ("y",), ("xy",), ("yx",)):
+                if (s, *name) in sums:
+                    sums[(s, *name)].wait_recv()
         size = quarter
         for c in range(2):
-            acc[s, c, 0] += fr[s, c, 0].astype(f32) + sr[s, c].astype(f32)
+            acc[s, 0, c] += fr[s, 0, c].astype(f32) + sr[s, c].astype(f32)
         base = 0
         for k in range(3, early):
             size = size // 2
             for c in range(2):
-                lt[s, c, base : base + size, :] = acc[s, c, 0, size : 2 * size, :].astype(bf16)
+                lt[s, c, base : base + size, :] = acc[s, 0, c, size : 2 * size, :].astype(bf16)
             view = pl.ds(base, size)
             copy = remote(lt.at[s, :, view], lr.at[s, :, view], 2**k)
             copy.wait_recv()
             for c in range(2):
-                acc[s, c, 0, :size, :] += lr[s, c, base : base + size, :].astype(f32)
+                acc[s, 0, c, :size, :] += lr[s, c, base : base + size, :].astype(f32)
             base += size
-        return jnp.concatenate([acc[s, c, 0, :size, :] for c in range(2)], axis=1)
+        return jnp.concatenate([acc[s, 0, c, :size, :] for c in range(2)], axis=1)
 
     late_factor = lh.at[:, pl.ds(0, late * rank)]
 
@@ -438,25 +467,27 @@
     urgent(0)
     g_send(1, "rest")
     rest(0)
-    for i in range(n // group):
-        weights(i * group, (i + 1) * group)
-        if i == 1:
-            with jax.named_scope("relay0"):
-                g_relay(1, "head")
+    places = n // group
+    for place in range(places):
+        weights(place, 1)
+    map_first(0, late_factor, (3, 2))
+    with jax.named_scope("relay0"):
+        g_relay(1, "head")
+    map_first(0, late_factor, (1, 0))
+    for place in range(places // 2):
+        weights(place, 0)
     for k in range(1, early):
-        if k > 1 and depth - 1 - k > late:
-            factors(k - 1)
         urgent(k)
         if k == 1:
-            map_first(0, late_factor, (3, 2))
             with jax.named_scope("relay1"):
                 g_relay(1, "rest")
-            map_first(0, late_factor, (1, 0))
-        else:
-            if depth - 1 - k <= late:
-                factors(k - 1)
-            rest(k - 1)
-    map_second(0, late_factor)
+            for place in range(places // 2, places):
+                weights(place, 0)
+            late_second((3, 2))
+        if k < early - 1:
+            rest(k)
+            factors(k)
+    late_second((1, 0))
 
     mine_cols = pl.ds(pl.multiple_of(par * half, half), half)
     other_cols = pl.ds(pl.multiple_of((1 - par) * half, half), half)
@@ -478,10 +509,11 @@
             forwards[m].wait_recv()
     finish(other_cols, [sibling(m) for m in range(late, depth)])
     map_first(1, co, (3, 2, 1, 0))
+    map_second((3, 2))
     rest(early - 1)
     factors(early - 1)
-    map_third(0)
-    map_second(1, co)
+    map_second((1, 0))
+    late_third()
     for k in range(early, depth):
         with jax.named_scope(f"turgent{k}"):
             t_wait(k, "rest")
@@ -490,9 +522,10 @@
             rest(k)
             factors(k)
         if k == early:
-            map_third(1)
-            corrections = map_fourth(0).astype(bf16)
-            partial = map_fourth(1)
+            map_third()
+            late_rest()
+    corrections = map_fourth(0).astype(bf16)
+    partial = map_fourth(1)
     for m in range(late):
         ps[m * rank : (m + 1) * rank, mine_cols] = own(m)
     with jax.named_scope("forwards2"):
@@ -513,8 +546,6 @@
         view = slice(l * rank, (l + 1) * rank)
         low = (bl_ref[l] - lh[:, view].astype(f32)).astype(bf16)
         xs[...] += mm(low, ps[view, :])
-    store = pltpu.make_async_copy(xs, out_hbm, store_sem.at[0])
-    store.start()
     result = prior_ref[...].astype(f32) + total[:tile]
     for v, copy in lines:
         with jax.named_scope(f"line{v}"):
@@ -522,27 +553,21 @@
         result = result + zr[v].astype(f32)
     map_ref[...] = result
     with jax.named_scope("end"):
-        store.wait()
         for copy in pool:
             copy.wait_send()
     assert len(arrivals) == recv_sem.shape[0], len(arrivals)
 
 
-def deliver(solved_ref, mapped_ref, out_ref, map_ref, held, spots, in_sem, out_sem):
-    piece = held.shape[0] // PIECES
-    moves = [(mapped_ref, spots, map_ref)]
+def deliver(solved_ref, mapped_ref, out_ref, map_ref, sems):
+    piece = solved_ref.shape[0] // PIECES
+    copies = [pltpu.make_async_copy(mapped_ref, map_ref, sems.at[PIECES])]
     for i in range(PIECES):
         view = pl.ds(i * piece, piece)
-        moves.append((solved_ref.at[view], held.at[view], out_ref.at[view]))
-    reads = [pltpu.make_async_copy(a, b, in_sem.at[i]) for i, (a, b, _) in enumerate(moves)]
-    writes = [pltpu.make_async_copy(b, c, out_sem.at[i]) for i, (_, b, c) in enumerate(moves)]
-    for read in reads:
-        read.start()
-    for read, write in zip(reads, writes):
-        read.wait()
-        write.start()
-    for write in writes:
-        write.wait()
+        copies.append(pltpu.make_async_copy(solved_ref.at[view], out_ref.at[view], sems.at[i]))
+    for copy in copies:
+        copy.start()
+    for copy in copies:
+        copy.wait()
 
 
 def body(
@@ -571,16 +596,13 @@
     line = 2**late
     early = depth - late
     products = sum((2 if m > 1 else 1) * (2 if depth - 1 - m in SPLIT else 1) for m in range(1, depth))
-    copies = line + 2 * early + late + depth + products + 2 * (early + 7) + line - 1
+    copies = line + 2 * early + late + depth + products + 18 + 2 * (early - 3) + line - 1
     quarter = n // 8 * tile
     solved, mapped = pl.pallas_call(
         functools.partial(kernel, n, leaf),
-        out_shape=(
-            jax.ShapeDtypeStruct((rows, samples), f32),
-            jax.ShapeDtypeStruct((tile, samples), f32),
-        ),
-        in_specs=[anywhere] * 9,
-        out_specs=(anywhere, vmem),
+        out_shape=(pltpu.VMEM((rows, samples), f32), pltpu.VMEM((tile, samples), f32)),
+        in_specs=[pl.BlockSpec(memory_space=pltpu.HBM)] * 9,
+        out_specs=(vmem, vmem),
         scratch_shapes=[
             pltpu.VMEM((rows, samples), bf16),
             pltpu.VMEM((rows, leaf), bf16),
@@ -591,7 +613,6 @@
             pltpu.VMEM((tile, samples), bf16),
             pltpu.SMEM((n, n), jnp.int32),
             pltpu.SMEM((n, n), jnp.int32),
-            pltpu.VMEM((rows, samples), f32),
             pltpu.VMEM((depth * rank, rows), bf16),
             pltpu.VMEM((rows, depth * rank), bf16),
             pltpu.VMEM((pair_total, rank, rank), f32),
@@ -619,21 +640,25 @@
             pltpu.SemaphoreType.DMA((SENDS,)),
             pltpu.SemaphoreType.DMA((copies,)),
             pltpu.SemaphoreType.DMA((2 * (levels - depth) + 9,)),
-            pltpu.SemaphoreType.DMA((1,)),
         ],
         compiler_params=pltpu.CompilerParams(
-            collective_id=0, has_side_effects=True, vmem_limit_bytes=60 * 1024 * 1024
+            collective_id=0, has_side_effects=True, vmem_limit_bytes=VMEM_LIMIT
         ),
     )(
-        residual_cols,
-        leaf_inverse,
-        basis_left,
-        basis_right,
-        point_pos.reshape(n, 1, rows),
-        map_pos.reshape(1, 1, tile),
-        prior_map,
-        block_first,
-        block_count,
+        *(
+            pltpu.with_memory_space_constraint(array, pltpu.HBM)
+            for array in (
+                residual_cols,
+                leaf_inverse,
+                basis_left,
+                basis_right,
+                point_pos.reshape(n, 1, rows),
+                map_pos.reshape(1, 1, tile),
+                prior_map,
+                block_first,
+                block_count,
+            )
+        )
     )
     return pl.pallas_call(
         deliver,
@@ -642,13 +667,9 @@
             jax.ShapeDtypeStruct((tile, samples), f32),
         ),
         in_specs=[anywhere] * 2,
-        out_specs=(anywhere, anywhere),
-        scratch_shapes=[
-            pltpu.VMEM((rows, samples), f32),
-            pltpu.VMEM((tile, samples), f32),
-            pltpu.SemaphoreType.DMA((PIECES + 1,)),
-            pltpu.SemaphoreType.DMA((PIECES + 1,)),
-        ],
+        out_specs=(pl.BlockSpec(memory_space=pltpu.HBM),) * 2,
+        scratch_shapes=[pltpu.SemaphoreType.DMA((PIECES + 1,))],
+        compiler_params=pltpu.CompilerParams(vmem_limit_bytes=1024 * 1024),
     )(solved, mapped)
 
 

time: 40.6 us -> 36.1 us (0.89)
  Pallas kernels: 39.8 us -> 35.3 us
    pallas_call x1, Pallas kernels: 37.9 us -> 34.4 us  [body(): pl.pallas_call(functools.partial(kernel, n, leaf), out_shape=(pltpu.VMEM(...]
    pallas_call x1, Pallas kernels: 1.87 us -> 0.85 us  [body(): pl.pallas_call(deliver, out_shape=(jax.ShapeDtypeStruct((rows, samples),...]
where the time goes in v2:
time: 36.1 us; the launch traced here: 35.9 us
  Pallas kernels  35.3 us (98%)
  between operations  0.64 us (2%)
    pallas_call x1, Pallas kernels, body(): pl.pallas_call(functools.partial(kernel, n, leaf), out_shape=(pltpu.VMEM(...  34.4 us
    pallas_call x1, Pallas kernels, body(): pl.pallas_call(deliver, out_shape=(jax.ShapeDtypeStruct((rows, samples),...  0.85 us

profile of v2, /device:TPU:0, one launch (start us, length us, event | category | flops | bytes accessed | tf_op | source)
XLA Modules:
  0.0 35.9 jit_solution(510398032040940081)
XLA Ops:
  0.6 34.4 %shard_map.104 = (f32[512,256]{1,0:T(8,128)S(1)}, f32[64,256]{1,0:T(8,128)S(1)}) custom-call(bf16[512,256]{1,0:T(8,128)(2,1)} %res_hbm.1, bf16[512,128]{1,0:T(8,128)(2,1)} %inv_hbm.1, f32[7,512,128]{2,1,0:T(8,128)} %bl_hbm.1, f32[7,512,128]{2,1,0:T(8,128)} %br_hbm.1, f32[32,1,512]{2,1,0:T(1,128)} %bitcast.2, f32[1,1,64]{2,1,0:T(1,128)} %bitcast.3, ...), custom_call_target="tpu_custom_call" | custom-call | tf_op jit(solution)/shard_map/pallas_call | solution.py:601
  35.1 0.9 %shard_map.105 = (f32[512,256]{1,0:T(8,128)}, f32[64,256]{1,0:T(8,128)}) custom-call(f32[512,256]{1,0:T(8,128)S(1)} %get-tuple-element.4.solved_ref, f32[64,256]{1,0:T(8,128)S(1)} %get-tuple-element.5.mapped_ref), custom_call_target="tpu_custom_call" | custom-call | tf_op jit(solution)/shard_map/pallas_call | solution.py:663

commit v3 on v2

--- a/solution.py
+++ b/solution.py
@@ -9,10 +9,9 @@
 
 AMPLITUDE = 0.2
 FAR = -1e6
-PIECES = 4
+PIECES = 2
 TOGETHER = 4
-SPLIT = (1,)
-SENDS = 17
+SENDS = 14
 VMEM_LIMIT = 50 * 1024 * 1024
 f32 = jnp.float32
 bf16 = jnp.bfloat16
@@ -69,6 +68,10 @@
     lr,
     zs,
     zr,
+    gz,
+    gy,
+    cown,
+    po,
     send_sem,
     recv_sem,
     load_sem,
@@ -105,15 +108,26 @@
             device_id_type=pl.DeviceIdType.MESH,
         )
 
+    def remote_all(src, dst, value):
+        recv = arrival()
+        for v in (3, 1, 2):
+            src[v] = value(v)
+            remote(src.at[v], dst.at[v], flips(v), recv)
+        view = pl.ds(1, 2**late - 1)
+        return describe(src.at[view], dst.at[view], 0, recv, 1)
+
+    def flips(v):
+        return sum(((v >> (late - 1 - i)) & 1) * 2 ** (early + i) for i in range(late))
+
     def arrival():
         arrivals.append(len(arrivals))
         return arrivals[-1]
 
-    def remote(src, dst, mask):
+    def remote(src, dst, mask, recv=None):
         slot = len(sends) % (len(pool) - 1) + 1
         if pool[slot] is not None:
             pool[slot].wait_send()
-        copy = describe(src, dst, slot, arrival(), mask)
+        copy = describe(src, dst, slot, arrival() if recv is None else recv, mask)
         copy.start()
         pool[slot] = copy
         sends.append(copy)
@@ -130,9 +144,10 @@
     tree = pl.ds(0, depth)
     load("r", br_hbm.at[tree], br_ref.at[tree])
     load("l", bl_hbm.at[tree], bl_ref.at[tree])
-    for l in range(levels - 1, depth - 1, -1):
-        load(("r", l), br_hbm.at[l], br_ref.at[l])
-        load(("l", l), bl_hbm.at[l], bl_ref.at[l])
+    if levels > depth:
+        own_levels = pl.ds(depth, levels - depth)
+        load("own_r", br_hbm.at[own_levels], br_ref.at[own_levels])
+        load("own_l", bl_hbm.at[own_levels], bl_ref.at[own_levels])
 
     barrier = pltpu.get_barrier_semaphore()
     for mask in range(1, n):
@@ -196,39 +211,22 @@
     pool[0] = describe(others, others, 0, 0, 1)
 
     g_copies = {}
-    relayed = set()
-    rank_half = rank // 2
-    core_rows = pl.ds(pl.multiple_of(par * rank_half, rank_half), rank_half)
 
     def g_span(k, part):
         m = depth - 1 - k
+        skip = late if k < early else 0
         if part == "head":
-            return g_off[k], m
+            return g_off[k] + skip, m - skip
         return g_off[k] + m, pairs[m] - m
 
     def g_send(k, part):
         start, size = g_span(k, part)
-        if size == 0:
-            return
-        span = pl.ds(start, size)
-        if k in SPLIT:
-            copy = remote(gs.at[span, core_rows], gr.at[span, core_rows], 2**k)
-        else:
-            copy = remote(gs.at[span], gr.at[span], 2**k)
-        g_copies[k, part] = copy
-
-    def g_relay(k, part):
-        start, size = g_span(k, part)
-        if k not in SPLIT or size == 0 or (k, part) in relayed:
-            return
-        relayed.add((k, part))
-        g_copies[k, part].wait_recv()
-        view = gr.at[pl.ds(start, size), core_rows]
-        g_copies[k, part] = remote(view, view, 1)
+        if size > 0:
+            span = pl.ds(start, size)
+            g_copies[k, part] = remote(gs.at[span], gr.at[span], 2**k)
 
     def g_wait(k, part):
         if (k, part) in g_copies:
-            g_relay(k, part)
             g_copies.pop((k, part)).wait_recv()
 
     def g_next(k):
@@ -244,9 +242,10 @@
     g_send(0, "head")
 
     total_rows = rows * n
+    if levels > depth:
+        loads["own_r"].wait()
+        loads["own_l"].wait()
     for level in range(levels - 1, depth - 1, -1):
-        loads["r", level].wait()
-        loads["l", level].wait()
         size = total_rows // 2 ** (level + 1)
         count = rows // size
         projected = []
@@ -257,11 +256,16 @@
         for a in range(count):
             view = slice(a * size, (a + 1) * size)
             xs[view, :] += mm(bl_ref[level, view, :].astype(bf16), projected[a ^ 1])
-    t_all = mm(rth[...], xs[...].astype(bf16))
-    for h in range(2):
-        t_half = t_all[:, h * half : (h + 1) * half].reshape(depth, rank, half)
-        tf[h] = t_half
-        ts[h, pl.ds(0, depth)] = t_half.astype(bf16)
+    right = xs[...].astype(bf16)
+
+    def project(low, high):
+        part = mm(rth[low * rank : high * rank, :], right)
+        for h in range(2):
+            t_half = part[:, h * half : (h + 1) * half].reshape(high - low, rank, half)
+            tf[h, low:high] = t_half
+            ts[h, low:high] = t_half.astype(bf16)
+
+    project(late, depth)
 
     top = depth - 1
     t_copies = {
@@ -269,8 +273,8 @@
             remote(ts.at[1 - par, pl.ds(late, depth - late)], tr.at[pl.ds(late, depth - late)], 1),
             remote(ts.at[par, top], cbuf.at[top, par], 1),
         ],
-        (0, "rest"): [remote(ts.at[1 - par, pl.ds(0, late)], tr.at[pl.ds(0, late)], 1)],
     }
+    project(0, late)
 
     def combine(k, low, high):
         m = depth - 1 - k
@@ -309,7 +313,7 @@
             with jax.named_scope(f"spot{place}"):
                 spots[place].wait_recv()
         start = place * group + core
-        own_u = pu[...]
+        own_u = pu[...] * (2.0 * leaf)
 
         def one(e):
             spot = 0
@@ -320,16 +324,15 @@
                 other = other + lax.rem(bit + bits[i], 2) * 2**i
             first = first_ref[other, me]
             last = first + count_ref[other, me]
-            t_col = jnp.broadcast_to(mpb[e], (128, 128)).T[:tile]
+            t_col = jnp.broadcast_to(mpb[e] * (2.0 * leaf), (128, 128)).T[:tile]
             base = pl.multiple_of(spot * tile, tile)
             for b in range(rows // leaf):
                 u_row = own_u[:, b * leaf : (b + 1) * leaf]
                 listed = jnp.logical_and(first <= b, b < last)
                 u_row = jnp.where(listed, u_row, FAR)
-                scaled = jnp.minimum(jnp.abs(t_col - u_row) * (2.0 * leaf), 1.0)
-                rest = 1.0 - scaled
-                square = rest * rest
-                value = AMPLITUDE * (square * square * (1.0 + 4.0 * scaled))
+                left = jnp.maximum(1.0 - jnp.abs(t_col - u_row), 0.0)
+                square = left * left
+                value = square * square * (5.0 * AMPLITUDE - 4.0 * AMPLITUDE * left)
                 wts[pl.ds(base, tile), b * leaf : (b + 1) * leaf] = value.astype(bf16)
 
         def several(i, carry):
@@ -344,79 +347,67 @@
     sums = {}
 
     def map_first(s, factor, order):
-        for j in order:
-            low = half_rows + j * quarter
-            ms[s, j] = mm(wts[low : low + quarter, :], factor[...]).astype(bf16)
-            sums[s, j] = remote(ms.at[s, j], mr.at[s, j], 1)
+        with jax.named_scope(f"mapfirst{s}{order[0]}"):
+            low, count = min(order), len(order)
+            rows_of = slice(half_rows + low * quarter, half_rows + (low + count) * quarter)
+            part = mm(wts[rows_of, :], factor[...])
+            ms[s, low : low + count] = part.astype(bf16).reshape(count, quarter, samples)
+            for j in order:
+                sums[s, j] = remote(ms.at[s, j], mr.at[s, j], 1)
+
+    kept = {}
 
     def keep(s, j, factor):
-        part = mm(wts[j * quarter : (j + 1) * quarter, :], factor[...])
+        if (s, j) not in kept:
+            low = j // 2 * 2
+            part = mm(wts[low * quarter : (low + 2) * quarter, :], factor[...])
+            kept[s, low], kept[s, low + 1] = part[:quarter], part[quarter:]
+        part = kept[s, j]
         with jax.named_scope(f"first{s}{j}"):
             sums[s, j].wait_recv()
         part = part + mr[s, j].astype(f32)
         return [part[:, c * half : (c + 1) * half] for c in range(2)]
 
-    def late_second(order):
+    def map_second(s, factor, order):
+        def to_x(slot, value):
+            fs[s, slot, 0] = value.astype(bf16)
+            sums[s, "x", slot] = remote(fs.at[s, slot, 0], fr.at[s, slot, 0], 2)
+
+        def to_y(slot, value):
+            fs[s, slot, 1] = value.astype(bf16)
+            sums[s, "y", slot] = remote(fs.at[s, slot, 1], fr.at[s, slot, 1], 4)
+
         for j in order:
-            part = keep(0, j, late_factor)
-            for c in range(2):
-                if j > 1:
-                    fs[0, j - 2, c] = part[c].astype(bf16)
-                else:
-                    acc[0, j, c] = part[c]
-            if j == 3:
-                sums[0, "x", 1] = remote(fs.at[0, 1], fr.at[0, 1], 2)
-            if j == 2:
-                sums[0, "x", 0] = remote(fs.at[0, 0, 0], fr.at[0, 0, 0], 2)
-
-    def late_rest():
-        sums[0, "x", 2] = remote(fs.at[0, 0, 1], fr.at[0, 0, 1], 2)
-
-    def late_third():
-        with jax.named_scope("third0"):
-            sums[0, "x", 1].wait_recv()
-        ss[0] = (acc[0, 1] + fr[0, 1].astype(f32)).astype(bf16)
-        sums[0, "y"] = remote(ss.at[0], sr.at[0], 4)
-
-    def map_second(order):
-        def to_x(slot, value):
-            fs[1, slot, 0] = value.astype(bf16)
-            sums[1, "x", slot] = remote(fs.at[1, slot, 0], fr.at[1, slot, 0], 2)
-
-        def to_y(slot, value):
-            fs[1, slot, 1] = value.astype(bf16)
-            sums[1, "y", slot] = remote(fs.at[1, slot, 1], fr.at[1, slot, 1], 4)
-
-        for j in order:
-            part = keep(1, j, co)
+            part = keep(s, j, factor)
             if j == 3:
                 to_x(1, part[0])
                 to_y(1, part[1])
             if j == 2:
                 to_x(0, part[0])
-                acc[1, 1, 1] = part[1]
+                acc[s, 1, 1] = part[1]
             if j == 1:
                 to_y(0, part[1])
-                acc[1, 1, 0] = part[0]
+                acc[s, 1, 0] = part[0]
             if j == 0:
                 for c in range(2):
-                    acc[1, 0, c] = part[c]
-
-    def map_third():
-        with jax.named_scope("third1"):
-            sums[1, "x", 1].wait_recv()
-        ss[1, 0] = (acc[1, 1, 0] + fr[1, 1, 0].astype(f32)).astype(bf16)
-        sums[1, "xy"] = remote(ss.at[1, 0], sr.at[1, 0], 4)
-        with jax.named_scope("thirdb1"):
-            sums[1, "y", 1].wait_recv()
-        ss[1, 1] = (acc[1, 1, 1] + fr[1, 1, 1].astype(f32)).astype(bf16)
-        sums[1, "yx"] = remote(ss.at[1, 1], sr.at[1, 1], 2)
+                    acc[s, 0, c] = part[c]
+
+    def map_third_x(s):
+        with jax.named_scope(f"third{s}"):
+            sums[s, "x", 1].wait_recv()
+        ss[s, 0] = (acc[s, 1, 0] + fr[s, 1, 0].astype(f32)).astype(bf16)
+        sums[s, "xy"] = remote(ss.at[s, 0], sr.at[s, 0], 4)
+
+    def map_third_y(s):
+        with jax.named_scope(f"thirdb{s}"):
+            sums[s, "y", 1].wait_recv()
+        ss[s, 1] = (acc[s, 1, 1] + fr[s, 1, 1].astype(f32)).astype(bf16)
+        sums[s, "yx"] = remote(ss.at[s, 1], sr.at[s, 1], 2)
 
     def map_fourth(s):
         with jax.named_scope(f"fourth{s}"):
-            for name in (("x", 0), ("x", 2), ("y", 0), ("y",), ("xy",), ("yx",)):
-                if (s, *name) in sums:
-                    sums[(s, *name)].wait_recv()
+            for name in ((s, "x", 0), (s, "y", 0), (s, "xy"), (s, "yx")):
+                sums[name].wait_recv()
         size = quarter
         for c in range(2):
             acc[s, 0, c] += fr[s, 0, c].astype(f32) + sr[s, c].astype(f32)
@@ -447,47 +438,67 @@
             combine(k, late, m)
             t_send(k + 1, late, m, "urgent")
 
-    def rest(k):
+    low_levels = pl.ds(0, late)
+
+    def correct(k, theirs):
+        g_mine = gs[g_off[k] : g_off[k] + late].reshape(late * rank, rank)
+        return mm(g_mine, theirs).reshape(late, rank, half)
+
+    def rest_send(k):
+        m = depth - 1 - k
+        theirs = tr[t_off[k] + m]
+        if k == 0:
+            away = tf[1 - par, low_levels] + correct(0, cbuf[top, 1 - par])
+            ts[1 - par, low_levels] = away.astype(bf16)
+            t_copies[0, "rest"] = [remote(ts.at[1 - par, low_levels], tr.at[low_levels], 1)]
+            tf[par, low_levels] += correct(0, theirs)
+        else:
+            total = tf[par, low_levels]
+            if k < early:
+                total = total + correct(k, theirs)
+                tf[par, low_levels] = total
+            ts[par, pl.ds(t_off[k], late)] = total.astype(bf16)
+            t_send(k, 0, late, "rest")
+
+    def rest_wait(k):
         with jax.named_scope(f"trest{k}"):
             t_wait(k, "rest")
-        with jax.named_scope(f"gheadb{k}"):
-            g_wait(k, "head")
-        combine(k, 0, min(late, depth - 1 - k))
-        t_send(k + 1, 0, min(late, depth - 1 - k), "rest")
+        tf[par, low_levels] += tr[pl.ds(t_off[k], late)].astype(f32)
 
     def factors(k):
         with jax.named_scope(f"gnext{k}"):
             g_next(k)
         g_send(k + 1, "head")
-        g_send(k + 1, "rest")
 
     with jax.named_scope("gnext0"):
         g_next(0)
     g_send(1, "head")
     urgent(0)
     g_send(1, "rest")
-    rest(0)
+    rest_send(0)
+
     places = n // group
-    for place in range(places):
+    near, far = range(places // 2), range(places // 2, places)
+    for core in (1, 0):
+        for place in near:
+            weights(place, core)
+    rest_wait(0)
+    urgent(1)
+    rest_send(1)
+    for place in far:
         weights(place, 1)
     map_first(0, late_factor, (3, 2))
-    with jax.named_scope("relay0"):
-        g_relay(1, "head")
     map_first(0, late_factor, (1, 0))
-    for place in range(places // 2):
+    for place in far:
         weights(place, 0)
-    for k in range(1, early):
+    for k in range(2, early):
+        if k == early - 1:
+            map_second(0, late_factor, (3, 2))
+        factors(k - 1)
+        g_send(k, "rest")
         urgent(k)
-        if k == 1:
-            with jax.named_scope("relay1"):
-                g_relay(1, "rest")
-            for place in range(places // 2, places):
-                weights(place, 0)
-            late_second((3, 2))
-        if k < early - 1:
-            rest(k)
-            factors(k)
-    late_second((1, 0))
+        rest_wait(k - 1)
+        rest_send(k)
 
     mine_cols = pl.ds(pl.multiple_of(par * half, half), half)
     other_cols = pl.ds(pl.multiple_of((1 - par) * half, half), half)
@@ -503,53 +514,76 @@
         ps[late * rank :, columns] = stacked
         co[:, columns] = (xs[:, columns] + mm(lh[:, late * rank :], stacked)).astype(bf16)
 
+    map_second(0, late_factor, (1, 0))
     finish(mine_cols, [own(m) for m in range(late, depth)])
     with jax.named_scope("forwards"):
         for m in range(late, depth - 1):
             forwards[m].wait_recv()
     finish(other_cols, [sibling(m) for m in range(late, depth)])
-    map_first(1, co, (3, 2, 1, 0))
-    map_second((3, 2))
-    rest(early - 1)
+    map_first(1, co, (3, 2))
+    map_first(1, co, (1, 0))
+    map_third_x(0)
+    map_third_y(0)
+    map_second(1, co, (3, 2))
+    rest_wait(early - 1)
+    rest_send(early)
     factors(early - 1)
-    map_second((1, 0))
-    late_third()
-    for k in range(early, depth):
+    map_second(1, co, (1, 0))
+
+    def late_step(k):
         with jax.named_scope(f"turgent{k}"):
             t_wait(k, "rest")
         forward(k)
         if k < depth - 1:
-            rest(k)
-            factors(k)
-        if k == early:
-            map_third()
-            late_rest()
-    corrections = map_fourth(0).astype(bf16)
-    partial = map_fourth(1)
-    for m in range(late):
+            with jax.named_scope(f"ghead{k}"):
+                g_wait(k, "head")
+            combine(k, 0, depth - 1 - k)
+            t_send(k + 1, 0, depth - 1 - k, "rest")
+
+    def gather(m):
+        with jax.named_scope(f"gather{m}"):
+            forwards[m].wait_recv()
         ps[m * rank : (m + 1) * rank, mine_cols] = own(m)
-    with jax.named_scope("forwards2"):
-        for m in range(late):
-            forwards[m].wait_recv()
-    for m in range(late):
         ps[m * rank : (m + 1) * rank, other_cols] = sibling(m)
-    total = partial + mm(corrections, ps[: late * rank])
-    lines = []
-    for v in (3, 1, 2):
-        mask = 0
-        for i in range(late):
-            mask += ((v >> (late - 1 - i)) & 1) * 2 ** (early + i)
-        zs[v] = total[v * tile : (v + 1) * tile].astype(bf16)
-        lines.append((v, remote(zs.at[v], zr.at[v], mask)))
-    xs[...] += mm(lh[...], ps[...])
-    for l in range(depth):
-        view = slice(l * rank, (l + 1) * rank)
-        low = (bl_ref[l] - lh[:, view].astype(f32)).astype(bf16)
-        xs[...] += mm(low, ps[view, :])
-    result = prior_ref[...].astype(f32) + total[:tile]
-    for v, copy in lines:
-        with jax.named_scope(f"line{v}"):
-            copy.wait_recv()
+
+    map_third_x(1)
+    late_step(early)
+    map_third_y(1)
+    last = ts.at[par, t_off[depth - 1]]
+    last_copy = remote(last, cown.at[par], 1)
+    plane = map_fourth(0).astype(bf16)
+    factor_lines = remote_all(gz, gy, lambda v: plane[v * tile : (v + 1) * tile, :rank])
+    gather(1)
+    total = mm(plane[:, rank:], ps[rank : 2 * rank, :])
+    total = map_fourth(1) + total
+    lines = remote_all(zs, zr, lambda v: total[v * tile : (v + 1) * tile].astype(bf16))
+
+    def settle(low, high):
+        rows_of = slice(low * rank, high * rank)
+        gained = mm(lh[:, rows_of], ps[rows_of, :])
+        for l in range(low, high):
+            view = slice(l * rank, (l + 1) * rank)
+            rest_of = (bl_ref[l] - lh[:, view].astype(f32)).astype(bf16)
+            gained = gained + mm(rest_of, ps[view, :])
+        xs[...] += gained
+
+    settle(1, depth)
+    late_step(depth - 1)
+    with jax.named_scope("last"):
+        last_copy.wait_recv()
+    po[:, mine_cols] = last[...]
+    po[:, other_cols] = cown[1 - par]
+    with jax.named_scope("factorlines"):
+        factor_lines.wait_recv()
+    near_factor = plane[:tile, :rank].astype(f32) + gy[2].astype(f32)
+    far_factor = gy[1].astype(f32) + gy[3].astype(f32)
+    gather(0)
+    tail = mm(near_factor.astype(bf16), ps[:rank, :]) + mm(far_factor.astype(bf16), po[...])
+    settle(0, 1)
+    result = prior_ref[...].astype(f32) + total[:tile] + tail
+    with jax.named_scope("lines"):
+        lines.wait_recv()
+    for v in range(1, 2**late):
         result = result + zr[v].astype(f32)
     map_ref[...] = result
     with jax.named_scope("end"):
@@ -595,8 +629,7 @@
     anywhere = pl.BlockSpec(memory_space=pl.ANY)
     line = 2**late
     early = depth - late
-    products = sum((2 if m > 1 else 1) * (2 if depth - 1 - m in SPLIT else 1) for m in range(1, depth))
-    copies = line + 2 * early + late + depth + products + 18 + 2 * (early - 3) + line - 1
+    copies = line + 4 * early + late + depth + 2 * (early + 7) + 3
     quarter = n // 8 * tile
     solved, mapped = pl.pallas_call(
         functools.partial(kernel, n, leaf),
@@ -637,9 +670,13 @@
             pltpu.VMEM((2, 2, quarter, half), bf16),
             pltpu.VMEM((line, tile, samples), bf16),
             pltpu.VMEM((line, tile, samples), bf16),
+            pltpu.VMEM((line, tile, rank), bf16),
+            pltpu.VMEM((line, tile, rank), bf16),
+            pltpu.VMEM((2, rank, half), bf16),
+            pltpu.VMEM((rank, samples), bf16),
             pltpu.SemaphoreType.DMA((SENDS,)),
             pltpu.SemaphoreType.DMA((copies,)),
-            pltpu.SemaphoreType.DMA((2 * (levels - depth) + 9,)),
+            pltpu.SemaphoreType.DMA((11 if levels > depth else 9,)),
         ],
         compiler_params=pltpu.CompilerParams(
             collective_id=0, has_side_effects=True, vmem_limit_bytes=VMEM_LIMIT

time: 36.1 us -> 34.1 us (0.945)
  Pallas kernels: 35.3 us -> 33.3 us
    pallas_call x1, Pallas kernels: 34.4 us -> 32.5 us  [body(): pl.pallas_call(functools.partial(kernel, n, leaf), out_shape=(pltpu.VMEM(...]
where the time goes in v3:
time: 34.1 us; the launch traced here: 34 us
  Pallas kernels  33.3 us (98%)
  between operations  0.64 us (2%)
    pallas_call x1, Pallas kernels, body(): pl.pallas_call(functools.partial(kernel, n, leaf), out_shape=(pltpu.VMEM(...  32.5 us
    pallas_call x1, Pallas kernels, body(): pl.pallas_call(deliver, out_shape=(jax.ShapeDtypeStruct((rows, samples),...  0.84 us

profile of v3, /device:TPU:0, one launch (start us, length us, event | category | flops | bytes accessed | tf_op | source)
XLA Modules:
  0.0 34.0 jit_solution(9339177905965912908)
XLA Ops:
  0.6 32.5 %shard_map.104 = (f32[512,256]{1,0:T(8,128)S(1)}, f32[64,256]{1,0:T(8,128)S(1)}) custom-call(bf16[512,256]{1,0:T(8,128)(2,1)} %res_hbm.1, bf16[512,128]{1,0:T(8,128)(2,1)} %inv_hbm.1, f32[7,512,128]{2,1,0:T(8,128)} %bl_hbm.1, f32[7,512,128]{2,1,0:T(8,128)} %br_hbm.1, f32[32,1,512]{2,1,0:T(1,128)} %bitcast.2, f32[1,1,64]{2,1,0:T(1,128)} %bitcast.3, ...), custom_call_target="tpu_custom_call" | custom-call | tf_op jit(solution)/shard_map/pallas_call | solution.py:634
  33.1 0.8 %shard_map.105 = (f32[512,256]{1,0:T(8,128)}, f32[64,256]{1,0:T(8,128)}) custom-call(f32[512,256]{1,0:T(8,128)S(1)} %get-tuple-element.4.solved_ref, f32[64,256]{1,0:T(8,128)S(1)} %get-tuple-element.5.mapped_ref), custom_call_target="tpu_custom_call" | custom-call | tf_op jit(solution)/shard_map/pallas_call | solution.py:700

commit v4 on v3

--- a/solution.py
+++ b/solution.py
@@ -104,31 +104,39 @@
             dst_ref=dst,
             send_sem=send_sem.at[send],
             recv_sem=recv_sem.at[recv],
-            device_id={"pts": partner(mask)},
+            device_id={"pts": partner(mask) if isinstance(mask, int) else mask},
             device_id_type=pl.DeviceIdType.MESH,
         )
 
-    def remote_all(src, dst, value):
+    def remote_all(src, dst, value, start=True):
         recv = arrival()
-        for v in (3, 1, 2):
+        copies = []
+        count = 2**late
+        for v in range(1, count):
             src[v] = value(v)
-            remote(src.at[v], dst.at[v], flips(v), recv)
-        view = pl.ds(1, 2**late - 1)
-        return describe(src.at[view], dst.at[view], 0, recv, 1)
-
-    def flips(v):
-        return sum(((v >> (late - 1 - i)) & 1) * 2 ** (early + i) for i in range(late))
+        here = me // 2**early
+        for step in range(1, count):
+            there = lax.rem(here + step, count)
+            device = me + (there - here) * 2**early
+            v = 0
+            for i in range(late):
+                differ = lax.rem(here // 2**i + there // 2**i, 2)
+                v = v + differ * 2 ** (late - 1 - i)
+            copies.append(remote(src.at[v], dst.at[v], device, recv, start))
+        view = pl.ds(1, count - 1)
+        return copies, describe(src.at[view], dst.at[view], 0, recv, 1)
 
     def arrival():
         arrivals.append(len(arrivals))
         return arrivals[-1]
 
-    def remote(src, dst, mask, recv=None):
+    def remote(src, dst, mask, recv=None, start=True):
         slot = len(sends) % (len(pool) - 1) + 1
         if pool[slot] is not None:
             pool[slot].wait_send()
         copy = describe(src, dst, slot, arrival() if recv is None else recv, mask)
-        copy.start()
+        if start:
+            copy.start()
         pool[slot] = copy
         sends.append(copy)
         return copy
@@ -479,14 +487,14 @@
 
     places = n // group
     near, far = range(places // 2), range(places // 2, places)
-    for core in (1, 0):
-        for place in near:
-            weights(place, core)
+    for place in range(places - 1):
+        weights(place, 1)
+    for place in near:
+        weights(place, 0)
+    weights(places - 1, 1)
     rest_wait(0)
     urgent(1)
     rest_send(1)
-    for place in far:
-        weights(place, 1)
     map_first(0, late_factor, (3, 2))
     map_first(0, late_factor, (1, 0))
     for place in far:
@@ -522,13 +530,13 @@
     finish(other_cols, [sibling(m) for m in range(late, depth)])
     map_first(1, co, (3, 2))
     map_first(1, co, (1, 0))
+    map_second(1, co, (3, 2))
     map_third_x(0)
     map_third_y(0)
-    map_second(1, co, (3, 2))
+    map_second(1, co, (1, 0))
     rest_wait(early - 1)
     rest_send(early)
     factors(early - 1)
-    map_second(1, co, (1, 0))
 
     def late_step(k):
         with jax.named_scope(f"turgent{k}"):
@@ -547,16 +555,26 @@
         ps[m * rank : (m + 1) * rank, other_cols] = sibling(m)
 
     map_third_x(1)
+    map_third_y(1)
     late_step(early)
-    map_third_y(1)
     last = ts.at[par, t_off[depth - 1]]
     last_copy = remote(last, cown.at[par], 1)
     plane = map_fourth(0).astype(bf16)
-    factor_lines = remote_all(gz, gy, lambda v: plane[v * tile : (v + 1) * tile, :rank])
+    _, factor_lines = remote_all(gz, gy, lambda v: plane[v * tile : (v + 1) * tile, :rank])
     gather(1)
     total = mm(plane[:, rank:], ps[rank : 2 * rank, :])
     total = map_fourth(1) + total
-    lines = remote_all(zs, zr, lambda v: total[v * tile : (v + 1) * tile].astype(bf16))
+    line_copies, lines = remote_all(
+        zs, zr, lambda v: total[v * tile : (v + 1) * tile].astype(bf16), start=False
+    )
+
+    def start_lines(core):
+        @pl.when(par == core)
+        def _():
+            for copy in line_copies:
+                copy.start()
+
+    start_lines(0)
 
     def settle(low, high):
         rows_of = slice(low * rank, high * rank)
@@ -569,6 +587,7 @@
 
     settle(1, depth)
     late_step(depth - 1)
+    start_lines(1)
     with jax.named_scope("last"):
         last_copy.wait_recv()
     po[:, mine_cols] = last[...]

time: 34.1 us -> 33.7 us (0.988)
    pallas_call x1, Pallas kernels: 32.5 us -> 32.1 us  [body(): pl.pallas_call(functools.partial(kernel, n, leaf), out_shape=(pltpu.VMEM(...]
where the time goes in v4:
time: 33.7 us; the launch traced here: 33.6 us
  Pallas kernels  33 us (98%)
  between operations  0.64 us (2%)
    pallas_call x1, Pallas kernels, body(): pl.pallas_call(functools.partial(kernel, n, leaf), out_shape=(pltpu.VMEM(...  32.1 us
    pallas_call x1, Pallas kernels, body(): pl.pallas_call(deliver, out_shape=(jax.ShapeDtypeStruct((rows, samples),...  0.84 us

profile of v4, /device:TPU:0, one launch (start us, length us, event | category | flops | bytes accessed | tf_op | source)
XLA Modules:
  0.0 33.6 jit_solution(17884990996274912980)
XLA Ops:
  0.6 32.1 %shard_map.104 = (f32[512,256]{1,0:T(8,128)S(1)}, f32[64,256]{1,0:T(8,128)S(1)}) custom-call(bf16[512,256]{1,0:T(8,128)(2,1)} %res_hbm.1, bf16[512,128]{1,0:T(8,128)(2,1)} %inv_hbm.1, f32[7,512,128]{2,1,0:T(8,128)} %bl_hbm.1, f32[7,512,128]{2,1,0:T(8,128)} %br_hbm.1, f32[32,1,512]{2,1,0:T(1,128)} %bitcast.2, f32[1,1,64]{2,1,0:T(1,128)} %bitcast.3, ...), custom_call_target="tpu_custom_call" | custom-call | tf_op jit(solution)/shard_map/pallas_call | solution.py:653
  32.8 0.8 %shard_map.105 = (f32[512,256]{1,0:T(8,128)}, f32[64,256]{1,0:T(8,128)}) custom-call(f32[512,256]{1,0:T(8,128)S(1)} %get-tuple-element.4.solved_ref, f32[64,256]{1,0:T(8,128)S(1)} %get-tuple-element.5.mapped_ref), custom_call_target="tpu_custom_call" | custom-call | tf_op jit(solution)/shard_map/pallas_call | solution.py:719

commit v5 on v4

--- a/solution.py
+++ b/solution.py
@@ -9,9 +9,9 @@
 
 AMPLITUDE = 0.2
 FAR = -1e6
-PIECES = 2
+PIECES = 1
 TOGETHER = 4
-SENDS = 14
+SENDS = 11
 VMEM_LIMIT = 50 * 1024 * 1024
 f32 = jnp.float32
 bf16 = jnp.bfloat16
@@ -122,7 +122,7 @@
             for i in range(late):
                 differ = lax.rem(here // 2**i + there // 2**i, 2)
                 v = v + differ * 2 ** (late - 1 - i)
-            copies.append(remote(src.at[v], dst.at[v], device, recv, start))
+            copies.append((there, remote(src.at[v], dst.at[v], device, recv, start)))
         view = pl.ds(1, count - 1)
         return copies, describe(src.at[view], dst.at[view], 0, recv, 1)
 
@@ -568,13 +568,15 @@
         zs, zr, lambda v: total[v * tile : (v + 1) * tile].astype(bf16), start=False
     )
 
-    def start_lines(core):
-        @pl.when(par == core)
-        def _():
-            for copy in line_copies:
-                copy.start()
-
-    start_lines(0)
+    @pl.when(par == 0)
+    def _():
+        for _, copy in line_copies:
+            copy.start()
+
+    def second_lines(first_place):
+        for there, copy in line_copies:
+            chosen = there == 0 if first_place else there > 0
+            pl.when(jnp.logical_and(par == 1, chosen))(copy.start)
 
     def settle(low, high):
         rows_of = slice(low * rank, high * rank)
@@ -587,13 +589,14 @@
 
     settle(1, depth)
     late_step(depth - 1)
-    start_lines(1)
+    second_lines(True)
     with jax.named_scope("last"):
         last_copy.wait_recv()
     po[:, mine_cols] = last[...]
     po[:, other_cols] = cown[1 - par]
     with jax.named_scope("factorlines"):
         factor_lines.wait_recv()
+    second_lines(False)
     near_factor = plane[:tile, :rank].astype(f32) + gy[2].astype(f32)
     far_factor = gy[1].astype(f32) + gy[3].astype(f32)
     gather(0)

time: 33.7 us -> 33.6 us (level)
  no operation moved by 1% of the time
where the time goes in v5:
time: 33.6 us; the launch traced here: 33.5 us
  Pallas kernels  32.8 us (98%)
  between operations  0.64 us (2%)
    pallas_call x1, Pallas kernels, body(): pl.pallas_call(functools.partial(kernel, n, leaf), out_shape=(pltpu.VMEM(...  32 us
    pallas_call x1, Pallas kernels, body(): pl.pallas_call(deliver, out_shape=(jax.ShapeDtypeStruct((rows, samples),...  0.83 us

profile of v5, /device:TPU:0, one launch (start us, length us, event | category | flops | bytes accessed | tf_op | source)
XLA Modules:
  0.0 33.5 jit_solution(14419144556173817342)
XLA Ops:
  0.6 32.0 %shard_map.104 = (f32[512,256]{1,0:T(8,128)S(1)}, f32[64,256]{1,0:T(8,128)S(1)}) custom-call(bf16[512,256]{1,0:T(8,128)(2,1)} %res_hbm.1, bf16[512,128]{1,0:T(8,128)(2,1)} %inv_hbm.1, f32[7,512,128]{2,1,0:T(8,128)} %bl_hbm.1, f32[7,512,128]{2,1,0:T(8,128)} %br_hbm.1, f32[32,1,512]{2,1,0:T(1,128)} %bitcast.2, f32[1,1,64]{2,1,0:T(1,128)} %bitcast.3, ...), custom_call_target="tpu_custom_call" | custom-call | tf_op jit(solution)/shard_map/pallas_call | solution.py:656
  32.6 0.8 %shard_map.105 = (f32[512,256]{1,0:T(8,128)}, f32[64,256]{1,0:T(8,128)}) custom-call(f32[512,256]{1,0:T(8,128)S(1)} %get-tuple-element.4.solved_ref, f32[64,256]{1,0:T(8,128)S(1)} %get-tuple-element.5.mapped_ref), custom_call_target="tpu_custom_call" | custom-call | tf_op jit(solution)/shard_map/pallas_call | solution.py:722
